TPU v7x, 512 devices: a whole 4x8x8 slice. The times are simulated.
512 devices in a mesh: seq: 128 (over y, z, core), head: 4 (over x).
Axes of the slice: x: 4, y: 8, z: 8, core: 2. Of those that a mesh axis runs over, the one named last changes fastest.
Arguments:
- queries: bfloat16 [32768, 2048], P('seq', 'head'), may hold values from -6 to 6
- key_rows: bfloat16 [32768, 2048], P('seq', 'head'), may hold values from -6 to 6
- value_rows: bfloat16 [32768, 2048], P('seq', 'head'), may hold values from -6 to 6
- out_gain: float32 [2048], P('head'), may hold values from 0.5 to 1.5
- doc_starts: int32 [1024], P('seq'), may hold values from 0 to 256, as said below
- doc_domains: int32 [1024], P('seq'), may hold values from 0 to 7
- domain_weights: int32 [8], replicated, may hold values from 1 to 8, as said below
- cotangent: bfloat16 [32768, 2048], P('seq', 'head'), may hold values from -0.3125 to 0.3125
- weight: float32 [2048, 2048], P('head', 'seq'), may hold values from -1.5 to 1.5
- moment_first: float32 [2048, 2048], P('head', 'seq'), may hold values from -6 to 6
- moment_second: float32 [2048, 2048], P('head', 'seq'), may hold values from 0.5 to 8
Outputs:
- attention: bfloat16 [32768, 2048], P('seq', 'head')
- new_weight: float32 [2048, 2048], P('head', 'seq')
- new_first: float32 [2048, 2048], P('head', 'seq')
- new_second: float32 [2048, 2048], P('head', 'seq')
Inputs may be any that keep to these rules, and one draw needn't show every extreme that they name: `doc_starts`: each block's 8 entries are ascending; entries below 256 are distinct start offsets and come first, entries equal to 256 mark unused slots. Some block uses all slots and has a start at offset 0, some block has no start, and most blocks have none. `domain_weights`: each of 1 to 8 once.
All inputs are finite; a program needn't handle non-finite values.
Results may differ from a plain program's by a relative error of at most 0.0049.
Values may be sent and summed in bfloat16 or wider, within the bound.
No kernel may reach another device: no remote copies, remote signals or barrier semaphores. Data moves between devices by JAX's collectives and lax.ppermute only.
A program may use at most 128 MiB of HBM per device.

v0:
```python
import jax
import jax.numpy as jnp
from jax import lax
from jax.sharding import PartitionSpec as P

HEAD_DIM = 128


first_debias = 0.9999734386011124
second_debias = 0.994079470779666


def carried_in(value, axis, combine, identity):
    peers, mine = (lax.axis_size(axis), lax.axis_index(axis))
    everything = jax.tree.map(lambda part: lax.all_gather(part, axis), value)
    start = jax.tree.map(
        lambda part, zero: jnp.broadcast_to(jnp.asarray(zero, part.dtype), part.shape),
        value,
        identity,
    )

    def hop(k, before):
        reached = k < mine
        new = combine(before, jax.tree.map(lambda part: part[k], everything))
        return jax.tree.map(lambda a, b: jnp.where(reached, a, b), new, before)

    return lax.fori_loop(0, peers, hop, start)


def local_docs(starts, row_count):
    positions = lax.broadcasted_iota(jnp.int32, (row_count, starts.shape[0]), 0)
    return jnp.sum((starts[None, :] <= positions).astype(jnp.int32), axis=1)


def shard_attention(queries, key_rows, value_rows, doc_local, carried, gain_vec, head_count):
    row_count = queries.shape[0]
    head_width = queries.shape[1] // head_count
    query_heads = queries.reshape(row_count, head_count, head_width)
    key_heads = key_rows.reshape(row_count, head_count, head_width)
    value_heads = value_rows.reshape(row_count, head_count, head_width)
    carried_half = carried.astype(jnp.bfloat16)
    scores = jnp.einsum("thd,shd->hts", query_heads, key_heads, preferred_element_type=jnp.float32)
    row_pos = lax.broadcasted_iota(jnp.int32, (row_count, row_count), 0) + 0
    col_pos = lax.broadcasted_iota(jnp.int32, (row_count, row_count), 1)
    visible = (col_pos <= row_pos) & (doc_local[:, None] == doc_local[None, :row_count])
    weights_half = jnp.where(visible[None], scores, 0.0).astype(jnp.bfloat16)
    inner_part = jnp.einsum(
        "hts,shd->thd", weights_half, value_heads, preferred_element_type=jnp.float32
    )
    carried_part = jnp.einsum(
        "thd,hde->the", query_heads, carried_half, preferred_element_type=jnp.float32
    )
    raw_sum = inner_part + jnp.where((doc_local == 0)[:, None, None], carried_part, 0.0)
    inv_scale = lax.rsqrt(jnp.mean(raw_sum * raw_sum, axis=2, keepdims=True) + 1e-05)
    normed = raw_sum * inv_scale * gain_vec.reshape(1, head_count, head_width)
    pieces = normed.astype(jnp.bfloat16).reshape(row_count, head_count * head_width)
    return pieces


def combine_apart(earlier, later):
    state_early, flag_early = earlier
    state_later, flag_later = later
    merged = state_later + (1.0 - flag_later) * state_early
    return (merged, jnp.maximum(flag_early, flag_later))


def on_device(
    queries,
    key_rows,
    value_rows,
    out_gain,
    doc_starts,
    doc_domains,
    domain_weights,
    cotangent,
    weight,
    moment_first,
    moment_second,
):
    row_count = queries.shape[0]
    head_count = out_gain.shape[0] // HEAD_DIM
    head_width = queries.shape[1] // head_count
    doc_local = local_docs(doc_starts, row_count)
    started = jnp.sum((doc_starts < row_count).astype(jnp.int32))
    slot_ids = lax.broadcasted_iota(jnp.int32, doc_starts.shape, 0)
    last_domain = jnp.sum(jnp.where(slot_ids == started - 1, doc_domains, 0))
    key_heads = key_rows.reshape(row_count, head_count, head_width)
    value_heads = value_rows.reshape(row_count, head_count, head_width)
    tail_keys = jnp.where(
        (doc_local == started)[:, None, None], key_heads, jnp.zeros_like(key_heads)
    )
    own_state = jnp.einsum(
        "thd,the->hde", tail_keys, value_heads, preferred_element_type=jnp.float32
    )
    flag_value = (started > 0).astype(jnp.float32)
    zero_state = jnp.zeros_like(own_state)
    zero_scalar = jnp.zeros((), jnp.float32)
    carried, flag_in = carried_in(
        (own_state, flag_value), "seq", combine_apart, (zero_state, zero_scalar)
    )
    summary = jnp.stack([started, last_domain]).reshape(1, 2)
    everyone = lax.all_gather(summary, "seq", axis=0, tiled=True)
    device_ids = lax.broadcasted_iota(jnp.int32, (everyone.shape[0],), 0)
    own_index = lax.axis_index("seq")
    latest = jnp.max(jnp.where((device_ids < own_index) & (everyone[:, 0] > 0), device_ids, -1))
    domain_in = jnp.sum(jnp.where(device_ids == latest, everyone[:, 1], 0))
    attention = shard_attention(
        queries, key_rows, value_rows, doc_local, carried, out_gain, head_count
    )
    looked_up = jnp.sum(
        jnp.where(doc_local[:, None] - 1 == slot_ids[None, :], doc_domains[None, :], 0), axis=1
    )
    token_domain = jnp.where(doc_local == 0, domain_in, looked_up)
    domain_ids = lax.broadcasted_iota(jnp.int32, (row_count, domain_weights.shape[0]), 1)
    token_weight = jnp.sum(
        jnp.where(token_domain[:, None] == domain_ids, domain_weights[None, :], 0), axis=1
    ).astype(jnp.float32)
    weighted = (cotangent.astype(jnp.float32) * token_weight[:, None]).astype(jnp.bfloat16)
    partial_grad = jnp.einsum(
        "tf,td->fd",
        attention,
        lax.all_gather(weighted, "head", axis=1, tiled=True),
        preferred_element_type=jnp.float32,
    )
    total_grad = lax.psum(partial_grad, "seq")
    owned_cols = weight.shape[1]
    gradient = lax.dynamic_slice_in_dim(
        total_grad, lax.axis_index("seq") * owned_cols, owned_cols, 1
    )
    new_first = 0.9 * moment_first + 0.1 * gradient
    new_second = 0.95 * moment_second + 0.05 * gradient * gradient
    corrected_first = new_first / first_debias
    corrected_second = new_second / second_debias
    new_weight = weight - 0.01 * (
        corrected_first / (jnp.sqrt(corrected_second) + 1e-08) + 0.1 * weight
    )
    return (attention, new_weight, new_first, new_second)


def solution(mesh):
    in_specs = (
        P("seq", "head"),
        P("seq", "head"),
        P("seq", "head"),
        P("head"),
        P("seq"),
        P("seq"),
        P(),
        P("seq", "head"),
        P("head", "seq"),
        P("head", "seq"),
        P("head", "seq"),
    )
    out_specs = (P("seq", "head"), P("head", "seq"), P("head", "seq"), P("head", "seq"))
    return jax.shard_map(
        on_device, mesh=mesh, in_specs=in_specs, out_specs=out_specs, check_vma=False
    )
```

profile of v0, /device:TPU:26, one launch (start us, length us, event | category | flops | bytes accessed | tf_op | source)
XLA Modules:
  0.0 831.2 jit_solution(6199093188138459606)
XLA Ops:
  7.2 1.3 fusion.26
  11.1 1.9 fusion.9
  13.7 1.3 dynamic-slice
  15.6 1.4 fusion.27
  16.9 1.5 add_dynamic-update-slice_fusion
  18.4 31.1 %all-reduce.1 = s32[256]{0:T(256)S(1)} all-reduce(s32[256]{0:T(256)S(1)} %add_dynamic-update-slice_fusion), channel_id=3, replica_groups=mesh['seq'=128,'head'=4] {'seq'}, use_global_device_ids=true, to_apply=%add.1 | all-reduce | flops 256 | bytes 2048
  50.6 1.3 fusion.28
  54.1 1.8 multiply_convert_fusion
  57.5 215.4 %all-reduce = f32[128]{0:T(128)S(1)} all-reduce(f32[128]{0:T(128)S(1)} %dynamic-update-slice), channel_id=1, replica_groups=mesh['seq'=128,'head'=4] {'seq'}, use_global_device_ids=true, to_apply=%add | all-reduce | flops 128 | bytes 1024
  272.8 308.3 %while.14 = (s32[]{:T(128)}, f32[4,128,128]{2,1,0:T(8,128)S(1)}, s32[]{:T(128)}, f32[128,4,128,128]{3,2,1,0:T(8,128)}, f32[128]{0:T(128)S(1)}, /*index=5*/s32[]{:T(128)}, f32[1]{0:T(128)}, s32[]{:T(128)}) while((s32[]{:T(128)}, f32[4,128,128]{2,1,0:T(8,128)S(1)}, s32[]{:T(128)}, f32[128,4,128,128]{3,2,1,0:T(8,128)}, ...), condition=%wide.region_3.4_spmd.clone, body=%wide.region_2.3_spmd.clone.sunk | while | flops 262149 | bytes 786569 | solution.py:27
  274.1 1.1 fusion.44
  276.5 1.1 fusion.44
  278.9 1.1 fusion.44
  281.3 1.1 fusion.44
  283.7 1.1 fusion.44
  286.1 1.1 fusion.44
  288.5 1.1 fusion.44
  291.0 1.1 fusion.44
  293.4 1.1 fusion.44
  295.8 1.1 fusion.44
  298.2 1.1 fusion.44
  300.6 1.1 fusion.44
  303.0 1.1 fusion.44
  305.4 1.1 fusion.44
  307.8 1.1 fusion.44
  310.2 1.1 fusion.44
  312.6 1.1 fusion.44
  315.0 1.1 fusion.44
  317.5 1.1 fusion.44
  319.9 1.1 fusion.44
  322.3 1.1 fusion.44
  324.7 1.1 fusion.44
  327.1 1.1 fusion.44
  329.5 1.1 fusion.44
  331.9 1.1 fusion.44
  334.3 1.1 fusion.44
  336.7 1.1 fusion.44
  339.1 1.1 fusion.44
  341.5 1.1 fusion.44
  344.0 1.1 fusion.44
  346.4 1.1 fusion.44
  348.8 1.1 fusion.44
  351.2 1.1 fusion.44
  353.6 1.1 fusion.44
  356.0 1.1 fusion.44
  358.4 1.1 fusion.44
  360.8 1.1 fusion.44
  363.2 1.1 fusion.44
  365.6 1.1 fusion.44
  368.0 1.1 fusion.44
  370.5 1.1 fusion.44
  372.9 1.1 fusion.44
  375.3 1.1 fusion.44
  377.7 1.1 fusion.44
  380.1 1.1 fusion.44
  382.5 1.1 fusion.44
  384.9 1.1 fusion.44
  430.7 1.1 fusion.44
  476.4 1.1 fusion.44
  522.2 1.1 fusion.44
  568.0 1.1 fusion.44
  582.2 3.9 fusion.35
  587.0 236.3 %all-reduce.4.cloned.1.call-done = f32[512,2048]{0,1:T(8,128)} async-done(((f32[512,2048]{0,1:T(8,128)}), f32[512,2048]{0,1:T(8,128)}) %all-reduce.4.cloned.1.call-update) | async-done | bytes 4194320 | tf_op jit(solution)/shard_map/psum | solution.py:125
  823.2 1.4 multiply_subtract_fusion
  (247 shorter events, 172.0 us)
Async XLA Ops:
  7.2 574.0 %copy-start = (bf16[256,512]{1,0:T(8,128)(2,1)S(1)}, bf16[256,512]{1,0:T(8,128)(2,1)}, u32[]{:S(2)}) copy-start(bf16[256,512]{1,0:T(8,128)(2,1)} %param.13) | copy-start | bytes 786436
  7.2 574.3 %copy-start.5 = (bf16[256,512]{1,0:T(8,128)(2,1)S(1)}, bf16[256,512]{1,0:T(8,128)(2,1)}, u32[]{:S(2)}) copy-start(bf16[256,512]{1,0:T(8,128)(2,1)} %param.15) | copy-start | bytes 786436
  7.2 265.6 %all-gather.7.cloned.1.call-start = ((), (), s32[]{:S(2)}) async-start(), calls=%async_computation.2 | async-start | bytes 33816576 | tf_op jit(solution)/shard_map/all_gather | solution.py:15
  13.0 569.2 %all-gather.5.cloned.1.call-start = ((), (), s32[]{:S(2)}) async-start(), calls=%async_computation | async-start | bytes 1310720 | tf_op jit(solution)/shard_map/all_gather | solution.py:122
  18.4 563.6 %copy-start.4 = (f32[512]{0:T(512)S(1)}, f32[512]{0:T(512)}, u32[]{:S(2)}) copy-start(f32[512]{0:T(512)} %param.16) | copy-start | bytes 6148
  55.9 767.4 %all-reduce.4.cloned.1.call-start = ((), (), s32[]{:S(2)}) async-start(), calls=%async_computation.1 | async-start | bytes 8388608 | tf_op jit(solution)/shard_map/psum | solution.py:125
  586.1 237.1 %copy-start.1 = (f32[512,16]{0,1:T(8,128)S(1)}, f32[512,16]{0,1:T(8,128)}, u32[]{:S(2)}) copy-start(f32[512,16]{0,1:T(8,128)} %param.21) | copy-start | bytes 98308
  586.1 237.1 %copy-start.2 = (f32[512,16]{0,1:T(8,128)S(1)}, f32[512,16]{0,1:T(8,128)}, u32[]{:S(2)}) copy-start(f32[512,16]{0,1:T(8,128)} %param.22) | copy-start | bytes 98308
  586.1 237.1 %copy-start.3 = (f32[512,16]{0,1:T(8,128)S(1)}, f32[512,16]{0,1:T(8,128)}, u32[]{:S(2)}) copy-start(f32[512,16]{0,1:T(8,128)} %param.23) | copy-start | bytes 98308
Sparse Core Ops, SparseCore 0:
  13.1 146.5 all-gather.6
  161.7 26.1 all-gather.4
  586.2 236.9 all-reduce.3
where the time goes:
time: 837 us; the launch traced here: 831 us
  blocking collectives  246 us (29%)
  waiting for transfers between devices  236 us (28%)
  other arithmetic  160 us (19%)
  loops' own time  86.3 us (10%)
  local copies, waits for them, and re-layouts  79.3 us (9%)
  between operations  15.9 us (2%)
    unnamed x2, blocking collectives  246 us
    psum x1, waiting for transfers between devices, on_device(): total_grad = lax.psum(partial_grad, 'seq')  236 us
    select_n x128, other arithmetic, hop(): return jax.tree.map(lambda a, b: jnp.where(reached, a, b), new, before)  147 us
    another operation x1, loops' own time, carried_in(): return lax.fori_loop(0, peers, hop, start)  86.3 us
    dynamic_slice x128, local copies, waits for them, and re-layouts, hop(): new = combine(before, jax.tree.map(lambda part: part[k], everything))  75 us
  transfers between devices with their start and end apart: 3, of which 1 were waited for; matrix products, arithmetic and copies ran while one was open for 28% of the time, Pallas kernels for 0%

commit v1 on v0

v1 whole, which is shorter than its diff:
```python
import jax
import jax.numpy as jnp
from jax import lax
from jax.experimental import pallas as pl
from jax.experimental.pallas import tpu as pltpu
from jax.sharding import Mesh, PartitionSpec as P

HEAD_DIM = 128
LANES = 128

first_debias = 0.9999734386011124
second_debias = 0.994079470779666

f32, bf16, i32 = jnp.float32, jnp.bfloat16, jnp.int32
VMEM_SPEC = pl.BlockSpec(memory_space=pltpu.VMEM)
SMEM_SPEC = pl.BlockSpec(memory_space=pltpu.SMEM)


def iota(shape, dim):
    return lax.broadcasted_iota(i32, shape, dim)


def docs_along(starts_ref, shape, dim):
    positions = iota(shape, dim)
    total = jnp.zeros(shape, i32)
    for slot in range(starts_ref.shape[0]):
        total = total + (starts_ref[slot] <= positions).astype(i32)
    return total


def started_and_domain(starts_ref, domains_ref, row_count):
    slots = starts_ref.shape[0]
    started = jnp.int32(0)
    for slot in range(slots):
        started = started + (starts_ref[slot] < row_count).astype(i32)
    last_domain = jnp.int32(0)
    for slot in range(slots):
        last_domain = last_domain + jnp.where(slot == started - 1, domains_ref[slot], 0)
    return started, last_domain


def dot(a, b, contract):
    return lax.dot_general(a, b, (contract, ((), ())), preferred_element_type=f32)


def state_kernel(key_ref, value_ref, starts_ref, domains_ref, out_ref):
    row_count, width = key_ref.shape
    started, last_domain = started_and_domain(starts_ref, domains_ref, row_count)
    in_tail = docs_along(starts_ref, (row_count, HEAD_DIM), 0) == started
    for head in range(width // HEAD_DIM):
        cols = slice(head * HEAD_DIM, (head + 1) * HEAD_DIM)
        keys = jnp.where(in_tail, key_ref[:, cols].astype(f32), 0.0).astype(bf16)
        out_ref[:, cols] = dot(keys, value_ref[:, cols], ((0,), (0,)))
    lane = iota((HEAD_DIM, LANES), 1)
    flag = (started > 0).astype(f32)
    out_ref[:, width:] = jnp.where(
        lane == 0, flag, jnp.where(lane == 1, last_domain.astype(f32), 0.0)
    )


def carry_kernel(own_ref, states_ref, carried_ref, domain_ref, *, width, rows):
    blocks = states_ref.shape[0]
    stride = width + LANES
    info = states_ref[:, width : width + LANES]
    flag_col = info[:, 0:1]
    domain_col = info[:, 1:2]
    here = iota((blocks, blocks), 0)
    there = iota((blocks, blocks), 1)
    flag_row = jnp.sum(jnp.where(here == there, flag_col, 0.0), axis=0, keepdims=True)
    latest = jnp.max(
        jnp.where((flag_row > 0.0) & (there < here), there, -1), axis=1, keepdims=True
    )
    joined = jnp.where((there < here) & (there >= latest), 1.0, 0.0).astype(bf16)
    for row in range(rows):
        state = states_ref[:, row * stride : row * stride + width]
        high = state.astype(bf16)
        rest = state - high.astype(f32)
        middle = rest.astype(bf16)
        low = (rest - middle.astype(f32)).astype(bf16)
        total = dot(joined, high, ((1,), (0,)))
        total = total + dot(joined, middle, ((1,), (0,)))
        total = total + dot(joined, low, ((1,), (0,)))
        carried_ref[:, row * width : (row + 1) * width] = total.astype(bf16)
    block_ids = iota((blocks, 1), 0)
    before = (flag_col > 0.0) & (block_ids < own_ref[0])
    last_block = jnp.max(jnp.where(before, block_ids, -1))
    domain_ref[0] = jnp.sum(jnp.where(block_ids == last_block, domain_col, 0.0)).astype(i32)


def inner_kernel(query_ref, key_ref, value_ref, starts_ref, out_ref):
    row_count, width = query_ref.shape
    square = (row_count, row_count)
    visible = (iota(square, 1) <= iota(square, 0)) & (
        docs_along(starts_ref, square, 0) == docs_along(starts_ref, square, 1)
    )
    for head in range(width // HEAD_DIM):
        cols = slice(head * HEAD_DIM, (head + 1) * HEAD_DIM)
        scores = dot(query_ref[:, cols], key_ref[:, cols], ((1,), (1,)))
        scores = jnp.where(visible, scores, 0.0).astype(bf16)
        out_ref[:, cols] = dot(scores, value_ref[:, cols], ((1,), (0,)))


def attention_kernel(
    query_ref, inner_ref, carried_ref, gain_ref, starts_ref, domains_ref, weights_ref,
    domain_in_ref, out_ref, shared_ref,
):
    row_count, width = query_ref.shape
    first_doc = docs_along(starts_ref, (row_count, HEAD_DIM), 0) == 0
    for head in range(width // HEAD_DIM):
        cols = slice(head * HEAD_DIM, (head + 1) * HEAD_DIM)
        part = dot(query_ref[:, cols], carried_ref[:, cols], ((1,), (0,)))
        raw = inner_ref[:, cols] + jnp.where(first_doc, part, 0.0)
        scale = lax.rsqrt(jnp.mean(raw * raw, axis=1, keepdims=True) + 1e-05)
        normed = (raw * scale * gain_ref[:, cols]).astype(bf16)
        out_ref[:, cols] = normed
        shared_ref[:row_count, cols] = normed
    doc = docs_along(starts_ref, (16, row_count), 1)
    domain = jnp.where(doc == 0, domain_in_ref[0], 0)
    for slot in range(starts_ref.shape[0]):
        domain = jnp.where(doc == slot + 1, domains_ref[slot], domain)
    weight = jnp.zeros((16, row_count), f32)
    for which in range(weights_ref.shape[0]):
        weight = jnp.where(domain == which, weights_ref[which].astype(f32), weight)
    shared_ref[row_count:, :row_count] = weight.astype(bf16)
    shared_ref[row_count:, row_count:] = jnp.zeros((16, width - row_count), bf16)


def turn_kernel(cotangent_ref, out_ref, *, owned):
    width = cotangent_ref.shape[1]
    turned = cotangent_ref[...].T
    for core in range(2):
        for pair in range(width // (2 * owned)):
            piece = turned[(2 * pair + core) * owned : (2 * pair + core + 1) * owned]
            for group in range(out_ref.shape[1]):
                out_ref[core, group, pair * owned : (pair + 1) * owned] = piece


def gradient_kernel(shared_ref, cotangent_ref, out_ref):
    cores, groups, cols, row_count = cotangent_ref.shape
    for group in range(groups):
        total = None
        for core in range(cores):
            weight = shared_ref[core, row_count : row_count + 1, :row_count].astype(f32)
            weighted = (cotangent_ref[core, group].astype(f32) * weight).astype(bf16)
            part = dot(weighted, shared_ref[core, :row_count, :], ((1,), (0,)))
            total = part if total is None else total + part
        out_ref[group * cols : (group + 1) * cols] = total.astype(bf16)


def update_kernel(
    parts_ref, weight_ref, first_ref, second_ref, new_weight_ref, new_first_ref, new_second_ref
):
    gradient = jnp.sum(parts_ref[...].astype(f32), axis=0)
    weight = weight_ref[...]
    new_first = 0.9 * first_ref[...] + 0.1 * gradient
    new_second = 0.95 * second_ref[...] + 0.05 * gradient * gradient
    corrected_first = new_first / first_debias
    corrected_second = new_second / second_debias
    new_first_ref[...] = new_first
    new_second_ref[...] = new_second
    new_weight_ref[...] = weight - 0.01 * (
        corrected_first / (jnp.sqrt(corrected_second) + 1e-08) + 0.1 * weight
    )


def shape(dims, dtype):
    return jax.ShapeDtypeStruct(dims, dtype)


def on_device(
    queries, key_rows, value_rows, out_gain, doc_starts, doc_domains, domain_weights,
    cotangent, weight, moment_first, moment_second,
):
    chips, groups = lax.axis_size("chip"), lax.axis_size("group")
    blocks = 2 * chips
    row_count, width = queries.shape
    owned = weight.shape[1]
    rows = HEAD_DIM // blocks
    own_block = (lax.axis_index("chip") * 2 + lax.axis_index("core")).reshape(1).astype(i32)
    V, S = VMEM_SPEC, SMEM_SPEC

    turned = pl.pallas_call(
        lambda c, o: turn_kernel(c, o, owned=owned),
        out_shape=shape((2, groups, width // 2, row_count), bf16),
        in_specs=[V], out_specs=V, name="turn",
    )(cotangent)
    states = pl.pallas_call(
        state_kernel,
        out_shape=shape((HEAD_DIM, width + LANES), f32),
        in_specs=[V, V, S, S], out_specs=V, name="state",
    )(key_rows, value_rows, doc_starts, doc_domains)
    states = states.reshape(blocks, rows * (width + LANES))
    states = lax.all_to_all(states, ("chip", "core"), 0, 0, tiled=True)
    turned = turned.reshape(2 * groups, width // 2, row_count)
    turned = lax.all_to_all(turned, ("core", "group"), 0, 0, tiled=True)
    turned = turned.reshape(2, groups, width // 2, row_count)
    inner = pl.pallas_call(
        inner_kernel,
        out_shape=shape((row_count, width), f32),
        in_specs=[V, V, V, S], out_specs=V, name="inner",
    )(queries, key_rows, value_rows, doc_starts)
    carried, domain_in = pl.pallas_call(
        lambda *refs: carry_kernel(*refs, width=width, rows=rows),
        out_shape=(shape((blocks, rows * width), bf16), shape((1,), i32)),
        in_specs=[S, V], out_specs=(V, S), name="carry",
    )(own_block, states)
    carried = lax.all_to_all(carried, ("chip", "core"), 0, 0, tiled=True)
    attention, shared = pl.pallas_call(
        attention_kernel,
        out_shape=(shape((row_count, width), bf16), shape((row_count + 16, width), bf16)),
        in_specs=[V, V, V, V, S, S, S, S], out_specs=(V, V), name="attention",
    )(
        queries, inner, carried.reshape(HEAD_DIM, width), out_gain.reshape(1, width),
        doc_starts, doc_domains, domain_weights, domain_in,
    )
    shared = lax.all_gather(shared, "core", axis=0, tiled=False)
    partial = pl.pallas_call(
        gradient_kernel,
        out_shape=shape((groups * width // 2, width), bf16),
        in_specs=[V, V], out_specs=V, name="gradient",
    )(shared, turned)
    partial = partial.reshape(chips, owned, width)
    partial = lax.all_to_all(partial, "chip", 0, 0, tiled=True)
    new_weight, new_first, new_second = pl.pallas_call(
        update_kernel,
        out_shape=(shape((owned, width), f32),) * 3,
        in_specs=[V] * 4, out_specs=(V,) * 3, name="update",
    )(partial, weight.T, moment_first.T, moment_second.T)
    return (attention, new_weight.T, new_first.T, new_second.T)


def solution(mesh):
    blocks, groups = mesh.devices.shape
    split = Mesh(mesh.devices.reshape(blocks // 2, 2, groups), ("chip", "core", "group"))
    seq, head = ("chip", "core"), "group"
    in_specs = (
        P(seq, head), P(seq, head), P(seq, head), P(head), P(seq), P(seq), P(),
        P(seq, head), P(head, seq), P(head, seq), P(head, seq),
    )
    out_specs = (P(seq, head), P(head, seq), P(head, seq), P(head, seq))
    return jax.shard_map(
        on_device, mesh=split, in_specs=in_specs, out_specs=out_specs, check_vma=False
    )
```

time: 837 us -> 126 us (0.15)
  the two profiles are of different devices: /device:TPU:26 before, /device:TPU:16 now
where the time goes in v1:
time: 126 us; the launch traced here: 125 us
  blocking collectives  41.9 us (33%)
  starting transfers between devices  29.8 us (24%)
  waiting for transfers between devices  28.4 us (23%)
  Pallas kernels  17.1 us (14%)
  local copies, waits for them, and re-layouts  5.79 us (5%)
  other arithmetic  1.58 us (1%)
    all_to_all x1, blocking collectives, on_device(): partial = lax.all_to_all(partial, 'chip', 0, 0, tiled=True)  37.7 us
    all_to_all x1, starting transfers between devices, on_device(): states = lax.all_to_all(states, ('chip', 'core'), 0, 0, tiled=True)  17.4 us
    all_to_all x1, waiting for transfers between devices, on_device(): states = lax.all_to_all(states, ('chip', 'core'), 0, 0, tiled=True)  14.5 us
    all_to_all x1, waiting for transfers between devices, on_device(): carried = lax.all_to_all(carried, ('chip', 'core'), 0, 0, tiled=True)  9.09 us
    all_to_all x1, starting transfers between devices, on_device(): carried = lax.all_to_all(carried, ('chip', 'core'), 0, 0, tiled=True)  8.13 us
    all_to_all x1, waiting for transfers between devices, on_device(): turned = lax.all_to_all(turned, ('core', 'group'), 0, 0, tiled=True)  4.73 us
    all_to_all x1, starting transfers between devices, on_device(): turned = lax.all_to_all(turned, ('core', 'group'), 0, 0, tiled=True)  4.32 us
    all_gather x1, blocking collectives, on_device(): shared = lax.all_gather(shared, 'core', axis=0, tiled=False)  4.16 us
  transfers between devices with their start and end apart: 3, of which 3 were waited for; matrix products, arithmetic and copies ran while one was open for 1% of the time, Pallas kernels for 6%

profile of v1, /device:TPU:16, one launch (start us, length us, event | category | flops | bytes accessed | tf_op | source)
XLA Modules:
  0.0 125.2 jit_solution(10173559629187002380)
XLA Ops:
  0.6 2.1 %state.1 = f32[128,640]{1,0:T(8,128)} custom-call(bf16[256,512]{1,0:T(8,128)(2,1)} %key_ref.3, bf16[256,512]{1,0:T(8,128)(2,1)} %value_ref.3, s32[8]{0:T(128)} %starts_ref.5, s32[8]{0:T(128)} %domains_ref.3), custom_call_target="tpu_custom_call" | custom-call | tf_op jit(solution)/shard_map/state/pallas_call | solution.py:187
  2.8 2.0 %copy.17 = f32[128,1,640]{2,1,0:T(1,128)} copy(f32[128,1,640]{2,0,1:T(8,128)} %bitcast.25) | data formatting | bytes 655360 | tf_op jit(solution)/shard_map/all_to_all | solution.py:193
  4.8 17.4 %all-to-all-start = ((f32[128,1,640]{2,1,0:T(1,128)}), f32[128,1,640]{2,1,0:T(1,128)S(1)}, u32[]{:S(2)}, u32[]{:S(2)}) async-start(f32[128,1,640]{2,1,0:T(1,128)} %copy.17), calls=%async_computation | async-start | bytes 655360 | tf_op jit(solution)/shard_map/all_to_all | solution.py:193
  22.2 14.5 %all-to-all-done = f32[128,1,640]{2,1,0:T(1,128)S(1)} async-done(((f32[128,1,640]{2,1,0:T(1,128)}), f32[128,1,640]{2,1,0:T(1,128)S(1)}, u32[]{:S(2)}, u32[]{:S(2)}) %all-to-all-start) | async-done | bytes 327712 | tf_op jit(solution)/shard_map/all_to_all | solution.py:193
  36.7 0.7 copy.23
  37.5 2.1 %carry.1 = (bf16[128,512]{1,0:T(8,128)(2,1)}, s32[1]{0:T(128)}) custom-call(s32[1]{0:T(128)} %bitcast.refs_0_, f32[128,640]{1,0:T(8,128)} %bitcast.24), custom_call_target="tpu_custom_call" | custom-call | tf_op jit(solution)/shard_map/carry/pallas_call | solution.py:202
  39.6 0.5 broadcast
  40.1 1.6 %reduce = bf16[128,512]{1,0:T(8,128)(2,1)S(1)} reduce(bf16[128,1,512]{2,0,1:T(8,128)(2,1)} %bitcast.27, bf16[]{:T(256)} %broadcast), dimensions={1}, to_apply=%copy.18.reduce_sub_computation | reduce | bytes 262146 | tf_op jit(solution)/shard_map/all_to_all | solution.py:207
  41.7 0.7 reshape.33
  42.4 8.1 %all-to-all-start.1 = ((bf16[128,2,256]{2,1,0:T(2,128)(2,1)}), bf16[128,2,256]{2,1,0:T(2,128)(2,1)S(1)}, u32[]{:S(2)}, u32[]{:S(2)}) async-start(bf16[128,2,256]{2,1,0:T(2,128)(2,1)} %reshape.33), calls=%async_computation.1 | async-start | bytes 262144 | tf_op jit(solution)/shard_map/all_to_all | solution.py:207
  50.5 2.1 %turn.1 = bf16[2,4,256,256]{3,2,1,0:T(8,128)(2,1)} custom-call(bf16[256,512]{1,0:T(8,128)(2,1)} %c.1), custom_call_target="tpu_custom_call" | custom-call | tf_op jit(solution)/shard_map/turn/pallas_call | solution.py:182
  52.6 9.1 %all-to-all-done.1 = bf16[128,2,256]{2,1,0:T(2,128)(2,1)S(1)} async-done(((bf16[128,2,256]{2,1,0:T(2,128)(2,1)}), bf16[128,2,256]{2,1,0:T(2,128)(2,1)S(1)}, u32[]{:S(2)}, u32[]{:S(2)}) %all-to-all-start.1) | async-done | bytes 131104 | tf_op jit(solution)/shard_map/all_to_all | solution.py:207
  61.7 4.3 %all-to-all-start.2 = ((bf16[8,256,256]{2,1,0:T(8,128)(2,1)}), bf16[8,256,256]{2,1,0:T(8,128)(2,1)S(1)}, u32[]{:S(2)}, u32[]{:S(2)}) async-start(bf16[8,256,256]{2,1,0:T(8,128)(2,1)} %bitcast.20), calls=%async_computation.2 | async-start | bytes 2097152 | tf_op jit(solution)/shard_map/all_to_all | solution.py:195
  66.0 2.6 %inner.1.inner_ref = f32[256,512]{1,0:T(8,128)} custom-call(bf16[256,512]{1,0:T(8,128)(2,1)} %query_ref.3, bf16[256,512]{1,0:T(8,128)(2,1)} %key_ref.3, bf16[256,512]{1,0:T(8,128)(2,1)} %value_ref.3, s32[8]{0:T(128)} %starts_ref.5), custom_call_target="tpu_custom_call" | custom-call | tf_op jit(solution)/shard_map/inner/pallas_call | solution.py:197
  68.6 0.1 reshape.34
  68.7 0.7 copy.24
  69.4 3.0 %attention.1 = (bf16[256,512]{1,0:T(8,128)(2,1)}, bf16[272,512]{1,0:T(8,128)(2,1)}) custom-call(bf16[256,512]{1,0:T(8,128)(2,1)} %query_ref.3, f32[256,512]{1,0:T(8,128)} %inner.1.inner_ref, bf16[128,512]{1,0:T(8,128)(2,1)} %bitcast.26, f32[1,512]{1,0:T(1,128)} %bitcast.31, s32[8]{0:T(128)} %starts_ref.5, s32[8]{0:T(128)} %domains_ref.3, s32[8]{0:T(128)} %weights_ref.1, ...), custom_call_target="tpu_custom_call" | custom-call | tf_op jit(solution)/shard_map/attention/pallas_call | solution.py:208
  72.4 4.2 %all-gather = bf16[544,512]{1,0:T(8,128)(2,1)} all-gather(bf16[272,512]{1,0:T(8,128)(2,1)} %get-tuple-element.14), channel_id=2, replica_groups=mesh['chip'=64,'core'=2,'group'=4] {'core'}, dimensions={0}, use_global_device_ids=true | all-gather | bytes 835584 | tf_op jit(solution)/shard_map/all_gather | solution.py:216
  76.5 4.7 %all-to-all-done.2 = bf16[8,256,256]{2,1,0:T(8,128)(2,1)S(1)} async-done(((bf16[8,256,256]{2,1,0:T(8,128)(2,1)}), bf16[8,256,256]{2,1,0:T(8,128)(2,1)S(1)}, u32[]{:S(2)}, u32[]{:S(2)}) %all-to-all-start.2) | async-done | bytes 1048608 | tf_op jit(solution)/shard_map/all_to_all | solution.py:195
  81.3 0.0 copy-start
  81.3 1.0 copy-done
  82.3 3.1 %gradient.1 = bf16[1024,512]{1,0:T(8,128)(2,1)} custom-call(bf16[2,272,512]{2,1,0:T(8,128)(2,1)} %bitcast.23, bf16[2,4,256,256]{3,2,1,0:T(8,128)(2,1)} %bitcast.21), custom_call_target="tpu_custom_call" | custom-call | tf_op jit(solution)/shard_map/gradient/pallas_call | solution.py:217
  85.4 37.7 %all_to_all.32.parts_ref = bf16[64,16,512]{2,1,0:T(8,128)(2,1)} all-to-all(bf16[64,16,512]{2,1,0:T(8,128)(2,1)} %bitcast.22), channel_id=1, replica_groups=mesh['chip'=64,'core'=2,'group'=4] {'chip'}, dimensions={0} | all-to-all | bytes 2097152 | tf_op jit(solution)/shard_map/all_to_all | solution.py:223
  123.1 2.1 %update.1 = (f32[16,512]{1,0:T(8,128)}, f32[16,512]{1,0:T(8,128)}, f32[16,512]{1,0:T(8,128)}) custom-call(bf16[64,16,512]{2,1,0:T(8,128)(2,1)} %all_to_all.32.parts_ref, f32[16,512]{1,0:T(8,128)} %bitcast.28, f32[16,512]{1,0:T(8,128)} %bitcast.29, f32[16,512]{1,0:T(8,128)} %bitcast.30), custom_call_target="tpu_custom_call" | custom-call | tf_op jit(solution)/shard_map/update/pallas_call | solution.py:224
Async XLA Ops:
  4.8 31.9 %all-to-all-start = ((f32[128,1,640]{2,1,0:T(1,128)}), f32[128,1,640]{2,1,0:T(1,128)S(1)}, u32[]{:S(2)}, u32[]{:S(2)}) async-start(f32[128,1,640]{2,1,0:T(1,128)} %copy.17), calls=%async_computation | async-start | bytes 655360 | tf_op jit(solution)/shard_map/all_to_all | solution.py:193
  42.4 19.3 %all-to-all-start.1 = ((bf16[128,2,256]{2,1,0:T(2,128)(2,1)}), bf16[128,2,256]{2,1,0:T(2,128)(2,1)S(1)}, u32[]{:S(2)}, u32[]{:S(2)}) async-start(bf16[128,2,256]{2,1,0:T(2,128)(2,1)} %reshape.33), calls=%async_computation.1 | async-start | bytes 262144 | tf_op jit(solution)/shard_map/all_to_all | solution.py:207
  61.7 19.6 %all-to-all-start.2 = ((bf16[8,256,256]{2,1,0:T(8,128)(2,1)}), bf16[8,256,256]{2,1,0:T(8,128)(2,1)S(1)}, u32[]{:S(2)}, u32[]{:S(2)}) async-start(bf16[8,256,256]{2,1,0:T(8,128)(2,1)} %bitcast.20), calls=%async_computation.2 | async-start | bytes 2097152 | tf_op jit(solution)/shard_map/all_to_all | solution.py:195
  81.3 1.0 copy-start

commit v2 on v1

--- a/solution.py
+++ b/solution.py
@@ -13,6 +13,7 @@
 
 f32, bf16, i32 = jnp.float32, jnp.bfloat16, jnp.int32
 VMEM_SPEC = pl.BlockSpec(memory_space=pltpu.VMEM)
+SMALL = pltpu.CompilerParams(vmem_limit_bytes=12 * 1024 * 1024)
 SMEM_SPEC = pl.BlockSpec(memory_space=pltpu.SMEM)
 
 
@@ -50,18 +51,19 @@
     for head in range(width // HEAD_DIM):
         cols = slice(head * HEAD_DIM, (head + 1) * HEAD_DIM)
         keys = jnp.where(in_tail, key_ref[:, cols].astype(f32), 0.0).astype(bf16)
-        out_ref[:, cols] = dot(keys, value_ref[:, cols], ((0,), (0,)))
+        out_ref[:, 0, cols] = dot(keys, value_ref[:, cols], ((0,), (0,)))
     lane = iota((HEAD_DIM, LANES), 1)
     flag = (started > 0).astype(f32)
-    out_ref[:, width:] = jnp.where(
+    out_ref[:, 0, width:] = jnp.where(
         lane == 0, flag, jnp.where(lane == 1, last_domain.astype(f32), 0.0)
     )
 
 
-def carry_kernel(own_ref, states_ref, carried_ref, domain_ref, *, width, rows):
-    blocks = states_ref.shape[0]
-    stride = width + LANES
-    info = states_ref[:, width : width + LANES]
+def carry_kernel(own_ref, states_ref, carried_ref, domain_ref, total_ref):
+    total, blocks = states_ref.shape[0], carried_ref.shape[0]
+    rows, heads = total // blocks, carried_ref.shape[1] // (total // blocks)
+    width = heads * HEAD_DIM
+    info = states_ref[0::rows, 0, width:] if rows > 1 else states_ref[:, 0, width:]
     flag_col = info[:, 0:1]
     domain_col = info[:, 1:2]
     here = iota((blocks, blocks), 0)
@@ -72,15 +74,18 @@
     )
     joined = jnp.where((there < here) & (there >= latest), 1.0, 0.0).astype(bf16)
     for row in range(rows):
-        state = states_ref[:, row * stride : row * stride + width]
-        high = state.astype(bf16)
-        rest = state - high.astype(f32)
-        middle = rest.astype(bf16)
-        low = (rest - middle.astype(f32)).astype(bf16)
-        total = dot(joined, high, ((1,), (0,)))
-        total = total + dot(joined, middle, ((1,), (0,)))
-        total = total + dot(joined, low, ((1,), (0,)))
-        carried_ref[:, row * width : (row + 1) * width] = total.astype(bf16)
+        for head in range(heads):
+            cols = slice(head * HEAD_DIM, (head + 1) * HEAD_DIM)
+            state = states_ref[row::rows, 0, cols] if rows > 1 else states_ref[:, 0, cols]
+            high = state.astype(bf16)
+            rest = state - high.astype(f32)
+            middle = rest.astype(bf16)
+            low = (rest - middle.astype(f32)).astype(bf16)
+            summed = dot(joined, high, ((1,), (0,)))
+            summed = summed + dot(joined, middle, ((1,), (0,)))
+            summed = summed + dot(joined, low, ((1,), (0,)))
+            total_ref[:, row * heads + head, :] = summed
+    carried_ref[...] = total_ref[...].astype(bf16)
     block_ids = iota((blocks, 1), 0)
     before = (flag_col > 0.0) & (block_ids < own_ref[0])
     last_block = jnp.max(jnp.where(before, block_ids, -1))
@@ -102,13 +107,15 @@
 
 def attention_kernel(
     query_ref, inner_ref, carried_ref, gain_ref, starts_ref, domains_ref, weights_ref,
-    domain_in_ref, out_ref, shared_ref,
+    domain_in_ref, out_ref, shared_ref, state_ref,
 ):
     row_count, width = query_ref.shape
     first_doc = docs_along(starts_ref, (row_count, HEAD_DIM), 0) == 0
+    state_ref[...] = carried_ref[...].astype(f32)
     for head in range(width // HEAD_DIM):
         cols = slice(head * HEAD_DIM, (head + 1) * HEAD_DIM)
-        part = dot(query_ref[:, cols], carried_ref[:, cols], ((1,), (0,)))
+        state = state_ref[:, head, :].astype(bf16)
+        part = dot(query_ref[:, cols], state, ((1,), (0,)))
         raw = inner_ref[:, cols] + jnp.where(first_doc, part, 0.0)
         scale = lax.rsqrt(jnp.mean(raw * raw, axis=1, keepdims=True) + 1e-05)
         normed = (raw * scale * gain_ref[:, cols]).astype(bf16)
@@ -125,26 +132,29 @@
     shared_ref[row_count:, row_count:] = jnp.zeros((16, width - row_count), bf16)
 
 
-def turn_kernel(cotangent_ref, out_ref, *, owned):
+def turn_kernel(cotangent_ref, core_ref, own_ref, other_ref, turned_ref, *, owned):
     width = cotangent_ref.shape[1]
-    turned = cotangent_ref[...].T
-    for core in range(2):
+    turned_ref[...] = cotangent_ref[...].T
+    for core, out_ref in ((core_ref[0], own_ref), (1 - core_ref[0], other_ref)):
         for pair in range(width // (2 * owned)):
-            piece = turned[(2 * pair + core) * owned : (2 * pair + core + 1) * owned]
-            for group in range(out_ref.shape[1]):
-                out_ref[core, group, pair * owned : (pair + 1) * owned] = piece
-
-
-def gradient_kernel(shared_ref, cotangent_ref, out_ref):
-    cores, groups, cols, row_count = cotangent_ref.shape
-    for group in range(groups):
+            start = pl.multiple_of(2 * pair * owned + core * owned, owned)
+            out_ref[pair * owned : (pair + 1) * owned] = turned_ref[pl.ds(start, owned), :]
+
+
+def gradient_kernel(place_ref, shared_ref, *refs):
+    cotangent_refs, out_ref = refs[:-1], refs[-1]
+    groups = len(cotangent_refs)
+    _, cols, row_count = cotangent_refs[0].shape
+    for shift, cotangent_ref in enumerate(cotangent_refs):
         total = None
-        for core in range(cores):
+        for side in range(2):
+            core = jnp.where(side == 0, place_ref[0], 1 - place_ref[0])
             weight = shared_ref[core, row_count : row_count + 1, :row_count].astype(f32)
-            weighted = (cotangent_ref[core, group].astype(f32) * weight).astype(bf16)
+            weighted = (cotangent_ref[side].astype(f32) * weight).astype(bf16)
             part = dot(weighted, shared_ref[core, :row_count, :], ((1,), (0,)))
             total = part if total is None else total + part
-        out_ref[group * cols : (group + 1) * cols] = total.astype(bf16)
+        group = lax.rem(place_ref[1] - shift + groups, groups)
+        out_ref[pl.ds(pl.multiple_of(group * cols, cols), cols), :] = total.astype(bf16)
 
 
 def update_kernel(
@@ -175,56 +185,66 @@
     blocks = 2 * chips
     row_count, width = queries.shape
     owned = weight.shape[1]
-    rows = HEAD_DIM // blocks
+    rows, heads = HEAD_DIM // blocks, width // HEAD_DIM
     own_block = (lax.axis_index("chip") * 2 + lax.axis_index("core")).reshape(1).astype(i32)
     V, S = VMEM_SPEC, SMEM_SPEC
 
-    turned = pl.pallas_call(
-        lambda c, o: turn_kernel(c, o, owned=owned),
-        out_shape=shape((2, groups, width // 2, row_count), bf16),
-        in_specs=[V], out_specs=V, name="turn",
-    )(cotangent)
+    place = jnp.stack([lax.axis_index("core"), lax.axis_index("group")]).astype(i32)
+    own_half, other_half = pl.pallas_call(
+        lambda *refs: turn_kernel(*refs, owned=owned),
+        out_shape=(shape((width // 2, row_count), bf16),) * 2,
+        in_specs=[V, S], out_specs=(V, V),
+        scratch_shapes=[pltpu.VMEM((width, row_count), bf16)],
+        compiler_params=SMALL, name="turn",
+    )(cotangent, place)
     states = pl.pallas_call(
         state_kernel,
-        out_shape=shape((HEAD_DIM, width + LANES), f32),
-        in_specs=[V, V, S, S], out_specs=V, name="state",
+        out_shape=shape((HEAD_DIM, 1, width + LANES), f32),
+        in_specs=[V, V, S, S], out_specs=V, compiler_params=SMALL, name="state",
     )(key_rows, value_rows, doc_starts, doc_domains)
-    states = states.reshape(blocks, rows * (width + LANES))
     states = lax.all_to_all(states, ("chip", "core"), 0, 0, tiled=True)
-    turned = turned.reshape(2 * groups, width // 2, row_count)
-    turned = lax.all_to_all(turned, ("core", "group"), 0, 0, tiled=True)
-    turned = turned.reshape(2, groups, width // 2, row_count)
+    partner_half = lax.ppermute(other_half, "core", [(0, 1), (1, 0)])
+    halves = jnp.stack([own_half, partner_half])
+    turned = [halves] + [
+        lax.ppermute(halves, "group", [(g, (g + k) % groups) for g in range(groups)])
+        for k in range(1, groups)
+    ]
     inner = pl.pallas_call(
         inner_kernel,
         out_shape=shape((row_count, width), f32),
-        in_specs=[V, V, V, S], out_specs=V, name="inner",
+        in_specs=[V, V, V, S], out_specs=V, compiler_params=SMALL, name="inner",
     )(queries, key_rows, value_rows, doc_starts)
     carried, domain_in = pl.pallas_call(
-        lambda *refs: carry_kernel(*refs, width=width, rows=rows),
-        out_shape=(shape((blocks, rows * width), bf16), shape((1,), i32)),
-        in_specs=[S, V], out_specs=(V, S), name="carry",
+        carry_kernel,
+        out_shape=(shape((blocks, rows * heads, HEAD_DIM), bf16), shape((1,), i32)),
+        in_specs=[S, V], out_specs=(V, S),
+        scratch_shapes=[pltpu.VMEM((blocks, rows * heads, HEAD_DIM), f32)],
+        compiler_params=SMALL, name="carry",
     )(own_block, states)
     carried = lax.all_to_all(carried, ("chip", "core"), 0, 0, tiled=True)
     attention, shared = pl.pallas_call(
         attention_kernel,
         out_shape=(shape((row_count, width), bf16), shape((row_count + 16, width), bf16)),
-        in_specs=[V, V, V, V, S, S, S, S], out_specs=(V, V), name="attention",
+        in_specs=[V, V, V, V, S, S, S, S], out_specs=(V, V),
+        scratch_shapes=[pltpu.VMEM((HEAD_DIM, heads, HEAD_DIM), f32)],
+        compiler_params=SMALL, name="attention",
     )(
-        queries, inner, carried.reshape(HEAD_DIM, width), out_gain.reshape(1, width),
+        queries, inner, carried.reshape(HEAD_DIM, heads, HEAD_DIM), out_gain.reshape(1, width),
         doc_starts, doc_domains, domain_weights, domain_in,
     )
     shared = lax.all_gather(shared, "core", axis=0, tiled=False)
     partial = pl.pallas_call(
         gradient_kernel,
         out_shape=shape((groups * width // 2, width), bf16),
-        in_specs=[V, V], out_specs=V, name="gradient",
-    )(shared, turned)
+        in_specs=[S] + [V] * (1 + groups), out_specs=V,
+        compiler_params=SMALL, name="gradient",
+    )(place, shared, *turned)
     partial = partial.reshape(chips, owned, width)
     partial = lax.all_to_all(partial, "chip", 0, 0, tiled=True)
     new_weight, new_first, new_second = pl.pallas_call(
         update_kernel,
         out_shape=(shape((owned, width), f32),) * 3,
-        in_specs=[V] * 4, out_specs=(V,) * 3, name="update",
+        in_specs=[V] * 4, out_specs=(V,) * 3, compiler_params=SMALL, name="update",
     )(partial, weight.T, moment_first.T, moment_second.T)
     return (attention, new_weight.T, new_first.T, new_second.T)
 

time: 126 us -> 116 us (0.921)
  waiting for transfers between devices: 28.4 us -> 16.6 us
  starting transfers between devices: 29.8 us -> 38.1 us
  Pallas kernels: 17.1 us -> 10.6 us
  blocking collectives: 41.9 us -> 45.5 us
  local copies, waits for them, and re-layouts: 5.79 us -> 3.91 us
  other arithmetic: 1.58 us -> 0.1 us
    ppermute x0 -> x4, starting transfers between devices: none -> 12.3 us  [the longest x3 10.3 us: on_device(): lax.ppermute(halves, 'group', [(g, (g + k) % groups) for g in range(group...]
    all_to_all x1, waiting for transfers between devices: 9.09 us -> 0.01 us  [on_device(): carried = lax.all_to_all(carried, ('chip', 'core'), 0, 0, tiled=True)]
    all_to_all x1, blocking collectives: 37.7 us -> 43.3 us  [on_device(): partial = lax.all_to_all(partial, 'chip', 0, 0, tiled=True)]
    ppermute x0 -> x4, waiting for transfers between devices: none -> 4.86 us  [the longest x3 4.86 us: on_device(): lax.ppermute(halves, 'group', [(g, (g + k) % groups) for g in range(group...]
    all_to_all x1 -> x0, waiting for transfers between devices: 4.73 us -> none  [on_device(): turned = lax.all_to_all(turned, ('core', 'group'), 0, 0, tiled=True)]
    all_to_all x1 -> x0, starting transfers between devices: 4.32 us -> none  [on_device(): turned = lax.all_to_all(turned, ('core', 'group'), 0, 0, tiled=True)]
    all_to_all x1, waiting for transfers between devices: 14.5 us -> 11.7 us  [on_device(): states = lax.all_to_all(states, ('chip', 'core'), 0, 0, tiled=True)]
    all_to_all x2 -> x0, local copies, waits for them, and re-layouts: 2.55 us -> none  [the longest x1 2.04 us: on_device(): states = lax.all_to_all(states, ('chip', 'core'), 0, 0, tiled=True)]
  transfers between devices with their start and end apart: 3 -> 6, of which waited for: 3 -> 3; matrix products, arithmetic and copies ran while one was open for 1% -> 0% of each run, Pallas kernels for 6% -> 6%
where the time goes in v2:
time: 116 us
  blocking collectives  45.5 us (39%)
  starting transfers between devices  38.1 us (33%)
  waiting for transfers between devices  16.6 us (14%)
  Pallas kernels  10.6 us (9%)
  local copies, waits for them, and re-layouts  3.91 us (3%)
    all_to_all x1, blocking collectives, on_device(): partial = lax.all_to_all(partial, 'chip', 0, 0, tiled=True)  43.3 us
    all_to_all x1, starting transfers between devices, on_device(): states = lax.all_to_all(states, ('chip', 'core'), 0, 0, tiled=True)  17.5 us
    all_to_all x1, waiting for transfers between devices, on_device(): states = lax.all_to_all(states, ('chip', 'core'), 0, 0, tiled=True)  11.7 us
    ppermute x3, starting transfers between devices, on_device(): lax.ppermute(halves, 'group', [(g, (g + k) % groups) for g in range(group...  10.3 us
    all_to_all x1, starting transfers between devices, on_device(): carried = lax.all_to_all(carried, ('chip', 'core'), 0, 0, tiled=True)  8.29 us
    ppermute x3, waiting for transfers between devices, on_device(): lax.ppermute(halves, 'group', [(g, (g + k) % groups) for g in range(group...  4.86 us
    unnamed x30, local copies, waits for them, and re-layouts  3.91 us
    pallas_call x1, Pallas kernels, on_device(): pl.pallas_call(attention_kernel, out_shape=(shape((row_count, width), bf1...  2.55 us
  transfers between devices with their start and end apart: 6, of which 3 were waited for; matrix products, arithmetic and copies ran while one was open for 0% of the time, Pallas kernels for 6%

profile of v2, /device:TPU:16, one launch (start us, length us, event | category | flops | bytes accessed | tf_op | source)
XLA Modules:
  0.0 115.6 jit_solution(17100089746439308085)
XLA Ops:
  0.6 0.0 copy-start.1
  0.6 0.9 copy-done.1
  1.6 0.0 copy-start.3
  1.6 0.9 copy-done.3
  2.5 0.0 copy-start.9
  2.5 0.7 copy-done.9
  3.2 0.0 copy-start.11
  3.2 0.7 copy-done.11
  3.8 1.7 %state.1 = f32[128,1,640]{2,1,0:T(1,128)} custom-call(bf16[256,512]{1,0:T(8,128)(2,1)S(1)} %copy-done.1, bf16[256,512]{1,0:T(8,128)(2,1)S(1)} %copy-done.3, s32[8]{0:T(128)S(1)} %copy-done.9, s32[8]{0:T(128)S(1)} %copy-done.11), custom_call_target="tpu_custom_call" | custom-call | tf_op jit(solution)/shard_map/state/pallas_call | solution.py:200
  5.6 0.0 copy-start.5
  5.6 17.5 %all-to-all-start = ((f32[128,1,640]{2,1,0:T(1,128)}), f32[128,1,640]{2,1,0:T(1,128)S(1)}, u32[]{:S(2)}, u32[]{:S(2)}) async-start(f32[128,1,640]{2,1,0:T(1,128)} %state.1), calls=%async_computation | async-start | bytes 655360 | tf_op jit(solution)/shard_map/all_to_all | solution.py:205
  23.1 0.1 pad_add_fusion.refs_1_.place_ref
  23.2 0.0 copy-done.5
  23.2 0.7 turn.1
  23.9 2.0 %collective-permute-start = (bf16[256,256]{1,0:T(8,128)(2,1)S(1)}, bf16[256,256]{1,0:T(8,128)(2,1)S(1)}, u32[]{:S(2)}, u32[]{:S(2)}) collective-permute-start(bf16[256,256]{1,0:T(8,128)(2,1)S(1)} %get-tuple-element.18), channel_id=1, source_target_pairs={{0,4},{4,0},{1,5},{5,1},{2,6},{6,2},{3,7},{7,3},{8,12},{12,8},{9,1... | collective-permute-start | bytes 393224 | tf_op jit(solution)/shard_map/ppermute | solution.py:206
  25.9 11.7 %all-to-all-done.states_ref = f32[128,1,640]{2,1,0:T(1,128)S(1)} async-done(((f32[128,1,640]{2,1,0:T(1,128)}), f32[128,1,640]{2,1,0:T(1,128)S(1)}, u32[]{:S(2)}, u32[]{:S(2)}) %all-to-all-start) | async-done | bytes 327712 | tf_op jit(solution)/shard_map/all_to_all | solution.py:205
  37.6 2.3 %carry.1 = (bf16[128,4,128]{2,1,0:T(4,128)(2,1)}, s32[1]{0:T(128)}) custom-call(s32[1]{0:T(128)} %bitcast.own_ref, f32[128,1,640]{2,1,0:T(1,128)S(1)} %all-to-all-done.states_ref), custom_call_target="tpu_custom_call" | custom-call | tf_op jit(solution)/shard_map/carry/pallas_call | solution.py:217
  39.9 0.0 copy-start.4
  39.9 0.0 copy-start.10
  40.0 8.3 %all-to-all-start.1 = ((bf16[128,4,128]{2,1,0:T(4,128)(2,1)}), bf16[128,4,128]{2,1,0:T(4,128)(2,1)S(1)}, u32[]{:S(2)}, u32[]{:S(2)}) async-start(bf16[128,4,128]{2,1,0:T(4,128)(2,1)} %get-tuple-element.13), calls=%async_computation.1 | async-start | bytes 262144 | tf_op jit(solution)/shard_map/all_to_all | solution.py:224
  48.2 0.0 collective-permute-done
  48.3 0.0 copy-start
  48.3 0.0 copy-start.2
  48.3 4.8 %collective-permute-start.3 = (bf16[2,256,256]{2,1,0:T(8,128)(2,1)S(1)}, bf16[2,256,256]{2,1,0:T(8,128)(2,1)S(1)}, u32[]{:S(2)}, u32[]{:S(2)}) collective-permute-start(bf16[2,256,256]{2,1,0:T(8,128)(2,1)S(1)} %pad_maximum_fusion.refs_0_), channel_id=1, source_target_pairs={{0,3},{1,0},{2,1},{3,2},{4,7},{5,4},{6,5},{7,6},{8,11},{9,8},{10,9... | collective-permute-start | bytes 786440 | tf_op jit(solution)/shard_map/ppermute | solution.py:209
  53.1 2.7 %collective-permute-start.2 = (bf16[2,256,256]{2,1,0:T(8,128)(2,1)S(1)}, bf16[2,256,256]{2,1,0:T(8,128)(2,1)S(1)}, u32[]{:S(2)}, u32[]{:S(2)}) collective-permute-start(bf16[2,256,256]{2,1,0:T(8,128)(2,1)S(1)} %pad_maximum_fusion.refs_0_), channel_id=1, source_target_pairs={{0,2},{1,3},{2,0},{3,1},{4,6},{5,7},{6,4},{7,5},{8,10},{9,11},{10,... | collective-permute-start | bytes 786440 | tf_op jit(solution)/shard_map/ppermute | solution.py:209
  55.8 2.8 %collective-permute-start.1 = (bf16[2,256,256]{2,1,0:T(8,128)(2,1)S(1)}, bf16[2,256,256]{2,1,0:T(8,128)(2,1)S(1)}, u32[]{:S(2)}, u32[]{:S(2)}) collective-permute-start(bf16[2,256,256]{2,1,0:T(8,128)(2,1)S(1)} %pad_maximum_fusion.refs_0_), channel_id=1, source_target_pairs={{0,1},{1,2},{2,3},{3,0},{4,5},{5,6},{6,7},{7,4},{8,9},{9,10},{10,1... | collective-permute-start | bytes 786440 | tf_op jit(solution)/shard_map/ppermute | solution.py:209
  58.6 0.0 copy-done.4
  58.6 0.0 copy-done.10
  58.7 0.0 copy-done
  58.7 0.0 copy-done.2
  58.7 1.2 %inner.1.inner_ref = f32[256,512]{1,0:T(8,128)S(1)} custom-call(bf16[256,512]{1,0:T(8,128)(2,1)S(1)} %copy-done, bf16[256,512]{1,0:T(8,128)(2,1)S(1)} %copy-done.2, bf16[256,512]{1,0:T(8,128)(2,1)S(1)} %copy-done.4, s32[8]{0:T(128)S(1)} %copy-done.10), custom_call_target="tpu_custom_call" | custom-call | tf_op jit(solution)/shard_map/inner/pallas_call | solution.py:212
  59.9 0.0 copy-start.13
  59.9 0.0 all-to-all-done.1.carried_ref
  59.9 0.0 copy-start.12
  59.9 0.0 copy-start.14
  59.9 0.6 copy-done.13
  60.6 0.0 copy-done.12
  60.6 0.0 copy-done.14
  60.6 2.5 %attention.1 = (bf16[256,512]{1,0:T(8,128)(2,1)}, bf16[272,512]{1,0:T(8,128)(2,1)S(1)}) custom-call(bf16[256,512]{1,0:T(8,128)(2,1)S(1)} %copy-done, f32[256,512]{1,0:T(8,128)S(1)} %inner.1.inner_ref, bf16[128,4,128]{2,1,0:T(4,128)(2,1)S(1)} %all-to-all-done.1.carried_ref, f32[1,512]{1,0:T(1,128)S(1)} %bitcast.20, s32[8]{0:T(128)S(1)} %copy-done.10, ...), custom_call_target="tpu_custom_call" | custom-call | tf_op jit(solution)/shard_map/attention/pallas_call | solution.py:225
  63.1 2.2 %all-gather = bf16[544,512]{1,0:T(8,128)(2,1)S(1)} all-gather(bf16[272,512]{1,0:T(8,128)(2,1)S(1)} %get-tuple-element.16), channel_id=2, replica_groups=mesh['chip'=64,'core'=2,'group'=4] {'core'}, dimensions={0}, use_global_device_ids=true | all-gather | bytes 835584 | tf_op jit(solution)/shard_map/all_gather | solution.py:235
  65.3 0.0 collective-permute-done.3.refs_3_
  65.3 0.4 collective-permute-done.2.refs_2_
  65.7 4.4 %collective-permute-done.1.refs_1_ = bf16[2,256,256]{2,1,0:T(8,128)(2,1)S(1)} collective-permute-done((bf16[2,256,256]{2,1,0:T(8,128)(2,1)S(1)}, bf16[2,256,256]{2,1,0:T(8,128)(2,1)S(1)}, u32[]{:S(2)}, u32[]{:S(2)}) %collective-permute-start.1) | collective-permute-done | bytes 262176 | tf_op jit(solution)/shard_map/ppermute | solution.py:209
  70.2 1.3 %gradient.1 = bf16[1024,512]{1,0:T(8,128)(2,1)S(1)} custom-call(s32[2]{0:T(128)S(1)} %pad_add_fusion.refs_1_.place_ref, bf16[2,272,512]{2,1,0:T(8,128)(2,1)S(1)} %bitcast.15, bf16[2,256,256]{2,1,0:T(8,128)(2,1)S(1)} %pad_maximum_fusion.refs_0_, bf16[2,256,256]{2,1,0:T(8,128)(2,1)S(1)} %collective-permute-done.1.refs_1_, ...), custom_call_target="tpu_custom_call" | custom-call | tf_op jit(solution)/shard_map/gradient/pallas_call | solution.py:236
  71.5 0.0 copy-start.6
  71.5 0.0 copy-start.7
  71.5 0.0 copy-start.8
  71.5 43.3 %all_to_all.15.parts_ref = bf16[64,16,512]{2,1,0:T(8,128)(2,1)S(1)} all-to-all(bf16[64,16,512]{2,1,0:T(8,128)(2,1)S(1)} %bitcast.14), channel_id=1, replica_groups=mesh['chip'=64,'core'=2,'group'=4] {'chip'}, dimensions={0} | all-to-all | bytes 2097152 | tf_op jit(solution)/shard_map/all_to_all | solution.py:243
  114.8 0.0 copy-done.6
  114.8 0.0 copy-done.7
  114.8 0.0 copy-done.8
  114.8 0.9 update.1
  (1 shorter events, 0.0 us)
Async XLA Ops:
  0.6 1.0 copy-start.1
  1.6 0.9 copy-start.3
  2.5 0.7 copy-start.9
  3.2 0.7 copy-start.11
  5.6 17.6 %copy-start.5 = (bf16[256,512]{1,0:T(8,128)(2,1)S(1)}, bf16[256,512]{1,0:T(8,128)(2,1)}, u32[]{:S(2)}) copy-start(bf16[256,512]{1,0:T(8,128)(2,1)} %refs_0_.1) | copy-start | bytes 786436
  5.6 32.0 %all-to-all-start = ((f32[128,1,640]{2,1,0:T(1,128)}), f32[128,1,640]{2,1,0:T(1,128)S(1)}, u32[]{:S(2)}, u32[]{:S(2)}) async-start(f32[128,1,640]{2,1,0:T(1,128)} %state.1), calls=%async_computation | async-start | bytes 655360 | tf_op jit(solution)/shard_map/all_to_all | solution.py:205
  23.9 24.4 %collective-permute-start = (bf16[256,256]{1,0:T(8,128)(2,1)S(1)}, bf16[256,256]{1,0:T(8,128)(2,1)S(1)}, u32[]{:S(2)}, u32[]{:S(2)}) collective-permute-start(bf16[256,256]{1,0:T(8,128)(2,1)S(1)} %get-tuple-element.18), channel_id=1, source_target_pairs={{0,4},{4,0},{1,5},{5,1},{2,6},{6,2},{3,7},{7,3},{8,12},{12,8},{9,1... | collective-permute-start | bytes 393224 | tf_op jit(solution)/shard_map/ppermute | solution.py:206
  39.9 18.7 %copy-start.4 = (bf16[256,512]{1,0:T(8,128)(2,1)S(1)}, bf16[256,512]{1,0:T(8,128)(2,1)}, u32[]{:S(2)}) copy-start(bf16[256,512]{1,0:T(8,128)(2,1)} %value_ref.3) | copy-start | bytes 786436
  39.9 18.7 %copy-start.10 = (s32[8]{0:T(128)S(1)}, s32[8]{0:T(128)}, u32[]{:S(2)}) copy-start(s32[8]{0:T(128)} %starts_ref.5) | copy-start | bytes 100
  40.0 20.0 %all-to-all-start.1 = ((bf16[128,4,128]{2,1,0:T(4,128)(2,1)}), bf16[128,4,128]{2,1,0:T(4,128)(2,1)S(1)}, u32[]{:S(2)}, u32[]{:S(2)}) async-start(bf16[128,4,128]{2,1,0:T(4,128)(2,1)} %get-tuple-element.13), calls=%async_computation.1 | async-start | bytes 262144 | tf_op jit(solution)/shard_map/all_to_all | solution.py:224
  48.3 10.4 %copy-start = (bf16[256,512]{1,0:T(8,128)(2,1)S(1)}, bf16[256,512]{1,0:T(8,128)(2,1)}, u32[]{:S(2)}) copy-start(bf16[256,512]{1,0:T(8,128)(2,1)} %query_ref.3) | copy-start | bytes 786436
  48.3 10.4 %copy-start.2 = (bf16[256,512]{1,0:T(8,128)(2,1)S(1)}, bf16[256,512]{1,0:T(8,128)(2,1)}, u32[]{:S(2)}) copy-start(bf16[256,512]{1,0:T(8,128)(2,1)} %key_ref.3) | copy-start | bytes 786436
  48.3 17.0 %collective-permute-start.3 = (bf16[2,256,256]{2,1,0:T(8,128)(2,1)S(1)}, bf16[2,256,256]{2,1,0:T(8,128)(2,1)S(1)}, u32[]{:S(2)}, u32[]{:S(2)}) collective-permute-start(bf16[2,256,256]{2,1,0:T(8,128)(2,1)S(1)} %pad_maximum_fusion.refs_0_), channel_id=1, source_target_pairs={{0,3},{1,0},{2,1},{3,2},{4,7},{5,4},{6,5},{7,6},{8,11},{9,8},{10,9... | collective-permute-start | bytes 786440 | tf_op jit(solution)/shard_map/ppermute | solution.py:209
  53.1 12.6 %collective-permute-start.2 = (bf16[2,256,256]{2,1,0:T(8,128)(2,1)S(1)}, bf16[2,256,256]{2,1,0:T(8,128)(2,1)S(1)}, u32[]{:S(2)}, u32[]{:S(2)}) collective-permute-start(bf16[2,256,256]{2,1,0:T(8,128)(2,1)S(1)} %pad_maximum_fusion.refs_0_), channel_id=1, source_target_pairs={{0,2},{1,3},{2,0},{3,1},{4,6},{5,7},{6,4},{7,5},{8,10},{9,11},{10,... | collective-permute-start | bytes 786440 | tf_op jit(solution)/shard_map/ppermute | solution.py:209
  55.8 14.4 %collective-permute-start.1 = (bf16[2,256,256]{2,1,0:T(8,128)(2,1)S(1)}, bf16[2,256,256]{2,1,0:T(8,128)(2,1)S(1)}, u32[]{:S(2)}, u32[]{:S(2)}) collective-permute-start(bf16[2,256,256]{2,1,0:T(8,128)(2,1)S(1)} %pad_maximum_fusion.refs_0_), channel_id=1, source_target_pairs={{0,1},{1,2},{2,3},{3,0},{4,5},{5,6},{6,7},{7,4},{8,9},{9,10},{10,1... | collective-permute-start | bytes 786440 | tf_op jit(solution)/shard_map/ppermute | solution.py:209
  59.9 0.7 copy-start.13
  59.9 0.7 copy-start.12
  59.9 0.7 copy-start.14
  71.5 43.3 %copy-start.6 = (f32[512,16]{0,1:T(8,128)S(1)}, f32[512,16]{0,1:T(8,128)}, u32[]{:S(2)}) copy-start(f32[512,16]{0,1:T(8,128)} %param.19) | copy-start | bytes 98308
  71.5 43.3 %copy-start.7 = (f32[512,16]{0,1:T(8,128)S(1)}, f32[512,16]{0,1:T(8,128)}, u32[]{:S(2)}) copy-start(f32[512,16]{0,1:T(8,128)} %param.20) | copy-start | bytes 98308
  71.5 43.3 %copy-start.8 = (f32[512,16]{0,1:T(8,128)S(1)}, f32[512,16]{0,1:T(8,128)}, u32[]{:S(2)}) copy-start(f32[512,16]{0,1:T(8,128)} %param.21) | copy-start | bytes 98308

commit v3 on v2

--- a/solution.py
+++ b/solution.py
@@ -5,6 +5,7 @@
 from jax.experimental.pallas import tpu as pltpu
 from jax.sharding import Mesh, PartitionSpec as P
 
+
 HEAD_DIM = 128
 LANES = 128
 
@@ -13,6 +14,7 @@
 
 f32, bf16, i32 = jnp.float32, jnp.bfloat16, jnp.int32
 VMEM_SPEC = pl.BlockSpec(memory_space=pltpu.VMEM)
+HBM_SPEC = pl.BlockSpec(memory_space=pltpu.HBM)
 SMALL = pltpu.CompilerParams(vmem_limit_bytes=12 * 1024 * 1024)
 SMEM_SPEC = pl.BlockSpec(memory_space=pltpu.SMEM)
 
@@ -44,7 +46,21 @@
     return lax.dot_general(a, b, (contract, ((), ())), preferred_element_type=f32)
 
 
-def state_kernel(key_ref, value_ref, starts_ref, domains_ref, out_ref):
+def state_kernel(
+    key_hbm, value_hbm, starts_hbm, domains_hbm, out_ref,
+    key_ref, value_ref, starts_ref, domains_ref, arrived,
+):
+    copies = [
+        pltpu.make_async_copy(source, target, arrived.at[which])
+        for which, (source, target) in enumerate((
+            (starts_hbm, starts_ref), (domains_hbm, domains_ref),
+            (key_hbm, key_ref), (value_hbm, value_ref),
+        ))
+    ]
+    for copy in copies:
+        copy.start()
+    for copy in copies:
+        copy.wait()
     row_count, width = key_ref.shape
     started, last_domain = started_and_domain(starts_ref, domains_ref, row_count)
     in_tail = docs_along(starts_ref, (row_count, HEAD_DIM), 0) == started
@@ -59,7 +75,7 @@
     )
 
 
-def carry_kernel(own_ref, states_ref, carried_ref, domain_ref, total_ref):
+def carry_kernel(own_ref, weights_ref, states_ref, carried_ref, weight_ref, total_ref):
     total, blocks = states_ref.shape[0], carried_ref.shape[0]
     rows, heads = total // blocks, carried_ref.shape[1] // (total // blocks)
     width = heads * HEAD_DIM
@@ -74,62 +90,72 @@
     )
     joined = jnp.where((there < here) & (there >= latest), 1.0, 0.0).astype(bf16)
     for row in range(rows):
+        state = states_ref[row::rows, 0, :width] if rows > 1 else states_ref[:, 0, :width]
+        high = state.astype(bf16)
+        rest = state - high.astype(f32)
+        middle = rest.astype(bf16)
+        low = (rest - middle.astype(f32)).astype(bf16)
+        summed = dot(joined, high, ((1,), (0,)))
+        summed = summed + dot(joined, middle, ((1,), (0,)))
+        summed = summed + dot(joined, low, ((1,), (0,)))
         for head in range(heads):
             cols = slice(head * HEAD_DIM, (head + 1) * HEAD_DIM)
-            state = states_ref[row::rows, 0, cols] if rows > 1 else states_ref[:, 0, cols]
-            high = state.astype(bf16)
-            rest = state - high.astype(f32)
-            middle = rest.astype(bf16)
-            low = (rest - middle.astype(f32)).astype(bf16)
-            summed = dot(joined, high, ((1,), (0,)))
-            summed = summed + dot(joined, middle, ((1,), (0,)))
-            summed = summed + dot(joined, low, ((1,), (0,)))
-            total_ref[:, row * heads + head, :] = summed
+            total_ref[:, row * heads + head, :] = summed[:, cols]
     carried_ref[...] = total_ref[...].astype(bf16)
     block_ids = iota((blocks, 1), 0)
     before = (flag_col > 0.0) & (block_ids < own_ref[0])
     last_block = jnp.max(jnp.where(before, block_ids, -1))
-    domain_ref[0] = jnp.sum(jnp.where(block_ids == last_block, domain_col, 0.0)).astype(i32)
-
-
-def inner_kernel(query_ref, key_ref, value_ref, starts_ref, out_ref):
+    domain = jnp.sum(jnp.where(block_ids == last_block, domain_col, 0.0)).astype(i32)
+    weight = jnp.int32(0)
+    for which in range(weights_ref.shape[0]):
+        weight = jnp.where(domain == which, weights_ref[which], weight)
+    weight_ref[0] = weight
+
+
+def inner_kernel(
+    query_ref, key_ref, value_ref, gain_ref, starts_ref, domains_ref, weights_ref,
+    out_ref, first_ref, lines_ref,
+):
     row_count, width = query_ref.shape
     square = (row_count, row_count)
-    visible = (iota(square, 1) <= iota(square, 0)) & (
-        docs_along(starts_ref, square, 0) == docs_along(starts_ref, square, 1)
-    )
+    down, along = docs_along(starts_ref, square, 0), docs_along(starts_ref, square, 1)
+    visible = (iota(square, 1) <= iota(square, 0)) & (down == along)
+    first_doc = down[:, :HEAD_DIM] == 0
     for head in range(width // HEAD_DIM):
         cols = slice(head * HEAD_DIM, (head + 1) * HEAD_DIM)
-        scores = dot(query_ref[:, cols], key_ref[:, cols], ((1,), (1,)))
+        query = query_ref[:, cols]
+        scores = dot(query, key_ref[:, cols], ((1,), (1,)))
         scores = jnp.where(visible, scores, 0.0).astype(bf16)
         out_ref[:, cols] = dot(scores, value_ref[:, cols], ((1,), (0,)))
+        first_ref[:, cols] = jnp.where(first_doc, query.astype(f32), 0.0).astype(bf16)
+    doc = docs_along(starts_ref, (1, row_count), 1)
+    line = jnp.zeros((1, row_count), i32)
+    for slot in range(starts_ref.shape[0]):
+        weight = jnp.int32(0)
+        for which in range(weights_ref.shape[0]):
+            weight = jnp.where(domains_ref[slot] == which, weights_ref[which], weight)
+        line = jnp.where(doc == slot + 1, weight, line)
+    lines_ref[...] = jnp.zeros(lines_ref.shape, f32)
+    lines_ref[0:1, :] = gain_ref[...]
+    lines_ref[1:2, :row_count] = line.astype(f32)
 
 
 def attention_kernel(
-    query_ref, inner_ref, carried_ref, gain_ref, starts_ref, domains_ref, weights_ref,
-    domain_in_ref, out_ref, shared_ref, state_ref,
-):
-    row_count, width = query_ref.shape
-    first_doc = docs_along(starts_ref, (row_count, HEAD_DIM), 0) == 0
+    first_ref, inner_ref, carried_ref, lines_ref, weight_in_ref, out_ref, shared_ref, state_ref
+):
+    row_count, width = first_ref.shape
     state_ref[...] = carried_ref[...].astype(f32)
     for head in range(width // HEAD_DIM):
         cols = slice(head * HEAD_DIM, (head + 1) * HEAD_DIM)
         state = state_ref[:, head, :].astype(bf16)
-        part = dot(query_ref[:, cols], state, ((1,), (0,)))
-        raw = inner_ref[:, cols] + jnp.where(first_doc, part, 0.0)
+        raw = inner_ref[:, cols] + dot(first_ref[:, cols], state, ((1,), (0,)))
         scale = lax.rsqrt(jnp.mean(raw * raw, axis=1, keepdims=True) + 1e-05)
-        normed = (raw * scale * gain_ref[:, cols]).astype(bf16)
+        normed = (raw * scale * lines_ref[0:1, cols]).astype(bf16)
         out_ref[:, cols] = normed
         shared_ref[:row_count, cols] = normed
-    doc = docs_along(starts_ref, (16, row_count), 1)
-    domain = jnp.where(doc == 0, domain_in_ref[0], 0)
-    for slot in range(starts_ref.shape[0]):
-        domain = jnp.where(doc == slot + 1, domains_ref[slot], domain)
-    weight = jnp.zeros((16, row_count), f32)
-    for which in range(weights_ref.shape[0]):
-        weight = jnp.where(domain == which, weights_ref[which].astype(f32), weight)
-    shared_ref[row_count:, :row_count] = weight.astype(bf16)
-    shared_ref[row_count:, row_count:] = jnp.zeros((16, width - row_count), bf16)
+    line = lines_ref[1:2, :]
+    line = jnp.where(line == 0.0, weight_in_ref[0].astype(f32), line)
+    shared_ref[row_count:, :] = jnp.broadcast_to(line, (16, width)).astype(bf16)
 
 
 def turn_kernel(cotangent_ref, core_ref, own_ref, other_ref, turned_ref, *, owned):
@@ -200,38 +226,50 @@
     states = pl.pallas_call(
         state_kernel,
         out_shape=shape((HEAD_DIM, 1, width + LANES), f32),
-        in_specs=[V, V, S, S], out_specs=V, compiler_params=SMALL, name="state",
-    )(key_rows, value_rows, doc_starts, doc_domains)
+        in_specs=[HBM_SPEC] * 4, out_specs=V,
+        scratch_shapes=[
+            pltpu.VMEM(key_rows.shape, bf16), pltpu.VMEM(value_rows.shape, bf16),
+            pltpu.SMEM(doc_starts.shape, i32), pltpu.SMEM(doc_domains.shape, i32),
+            pltpu.SemaphoreType.DMA((4,)),
+        ],
+        compiler_params=SMALL, name="state",
+    )(*(
+        pltpu.with_memory_space_constraint(operand, pltpu.HBM)
+        for operand in (key_rows, value_rows, doc_starts, doc_domains)
+    ))
     states = lax.all_to_all(states, ("chip", "core"), 0, 0, tiled=True)
     partner_half = lax.ppermute(other_half, "core", [(0, 1), (1, 0)])
     halves = jnp.stack([own_half, partner_half])
-    turned = [halves] + [
-        lax.ppermute(halves, "group", [(g, (g + k) % groups) for g in range(groups)])
-        for k in range(1, groups)
-    ]
-    inner = pl.pallas_call(
+    turned = [halves]
+    for k in range(1, groups):
+        turned.append(lax.ppermute(halves, "group", [(g, (g + k) % groups) for g in range(groups)]))
+    inner, first, lines = pl.pallas_call(
         inner_kernel,
-        out_shape=shape((row_count, width), f32),
-        in_specs=[V, V, V, S], out_specs=V, compiler_params=SMALL, name="inner",
-    )(queries, key_rows, value_rows, doc_starts)
-    carried, domain_in = pl.pallas_call(
+        out_shape=(
+            shape((row_count, width), f32), shape((row_count, width), bf16), shape((8, width), f32)
+        ),
+        in_specs=[V, V, V, V, S, S, S], out_specs=(V, V, V),
+        compiler_params=SMALL, name="inner",
+    )(
+        queries, key_rows, value_rows, out_gain.reshape(1, width),
+        doc_starts, doc_domains, domain_weights,
+    )
+    carry_call = pl.pallas_call(
         carry_kernel,
         out_shape=(shape((blocks, rows * heads, HEAD_DIM), bf16), shape((1,), i32)),
-        in_specs=[S, V], out_specs=(V, S),
+        in_specs=[S, S, V], out_specs=(V, S),
         scratch_shapes=[pltpu.VMEM((blocks, rows * heads, HEAD_DIM), f32)],
         compiler_params=SMALL, name="carry",
-    )(own_block, states)
+    )
+    carried, weight_in = carry_call(own_block, domain_weights, states)
     carried = lax.all_to_all(carried, ("chip", "core"), 0, 0, tiled=True)
     attention, shared = pl.pallas_call(
         attention_kernel,
         out_shape=(shape((row_count, width), bf16), shape((row_count + 16, width), bf16)),
-        in_specs=[V, V, V, V, S, S, S, S], out_specs=(V, V),
+        in_specs=[V, V, V, V, S], out_specs=(V, V),
         scratch_shapes=[pltpu.VMEM((HEAD_DIM, heads, HEAD_DIM), f32)],
         compiler_params=SMALL, name="attention",
-    )(
-        queries, inner, carried.reshape(HEAD_DIM, heads, HEAD_DIM), out_gain.reshape(1, width),
-        doc_starts, doc_domains, domain_weights, domain_in,
-    )
+    )(first, inner, carried.reshape(HEAD_DIM, heads, HEAD_DIM), lines, weight_in)
     shared = lax.all_gather(shared, "core", axis=0, tiled=False)
     partial = pl.pallas_call(
         gradient_kernel,

time: 116 us -> 114 us (0.983)
  local copies, waits for them, and re-layouts: 3.91 us -> 0.07 us
  waiting for transfers between devices: 16.6 us -> 17.8 us
    unnamed x30 -> x22, local copies, waits for them, and re-layouts: 3.91 us -> 0.07 us
    ppermute x3, waiting for transfers between devices: 4.86 us -> 6.12 us  [on_device(): lax.ppermute(halves, 'group', [(g, (g + k) % groups) for g in range(group...]
  transfers between devices with their start and end apart: 6 -> 6, of which waited for: 3 -> 4; matrix products, arithmetic and copies ran while one was open for 0% -> 0% of each run, Pallas kernels for 6% -> 6%
where the time goes in v3:
time: 114 us
  blocking collectives  45.5 us (40%)
  starting transfers between devices  38.1 us (33%)
  waiting for transfers between devices  17.8 us (16%)
  Pallas kernels  11.4 us (10%)
    all_to_all x1, blocking collectives, on_device(): partial = lax.all_to_all(partial, 'chip', 0, 0, tiled=True)  43.3 us
    all_to_all x1, starting transfers between devices, on_device(): states = lax.all_to_all(states, ('chip', 'core'), 0, 0, tiled=True)  17.5 us
    all_to_all x1, waiting for transfers between devices, on_device(): states = lax.all_to_all(states, ('chip', 'core'), 0, 0, tiled=True)  11.7 us
    ppermute x3, starting transfers between devices, on_device(): lax.ppermute(halves, 'group', [(g, (g + k) % groups) for g in range(group...  10.3 us
    all_to_all x1, starting transfers between devices, on_device(): carried = lax.all_to_all(carried, ('chip', 'core'), 0, 0, tiled=True)  8.29 us
    ppermute x3, waiting for transfers between devices, on_device(): lax.ppermute(halves, 'group', [(g, (g + k) % groups) for g in range(group...  6.12 us
    pallas_call x1, Pallas kernels, on_device(): carried, weight_in = carry_call(own_block, domain_weights, states)  3.18 us
  transfers between devices with their start and end apart: 6, of which 4 were waited for; matrix products, arithmetic and copies ran while one was open for 0% of the time, Pallas kernels for 6%

profile of v3, /device:TPU:16, one launch (start us, length us, event | category | flops | bytes accessed | tf_op | source)
XLA Modules:
  0.0 113.9 jit_solution(15919527918839237806)
XLA Ops:
  0.6 2.3 %state.1 = f32[128,1,640]{2,1,0:T(1,128)} custom-call(bf16[256,512]{1,0:T(8,128)(2,1)} %key_hbm.1, bf16[256,512]{1,0:T(8,128)(2,1)} %value_hbm.1, s32[8]{0:T(128)} %starts_hbm.1, s32[8]{0:T(128)} %domains_hbm.1), custom_call_target="tpu_custom_call" | custom-call | tf_op jit(solution)/shard_map/state/pallas_call | solution.py:226
  2.9 0.0 copy-start.2
  2.9 17.5 %all-to-all-start = ((f32[128,1,640]{2,1,0:T(1,128)}), f32[128,1,640]{2,1,0:T(1,128)S(1)}, u32[]{:S(2)}, u32[]{:S(2)}) async-start(f32[128,1,640]{2,1,0:T(1,128)} %state.1), calls=%async_computation | async-start | bytes 655360 | tf_op jit(solution)/shard_map/all_to_all | solution.py:240
  20.4 0.1 pad_add_fusion.refs_1_.place_ref
  20.5 0.0 copy-done.2
  20.5 0.7 turn.1
  21.2 2.0 %collective-permute-start = (bf16[256,256]{1,0:T(8,128)(2,1)S(1)}, bf16[256,256]{1,0:T(8,128)(2,1)S(1)}, u32[]{:S(2)}, u32[]{:S(2)}) collective-permute-start(bf16[256,256]{1,0:T(8,128)(2,1)S(1)} %get-tuple-element.24), channel_id=1, source_target_pairs={{0,4},{4,0},{1,5},{5,1},{2,6},{6,2},{3,7},{7,3},{8,12},{12,8},{9,1... | collective-permute-start | bytes 393224 | tf_op jit(solution)/shard_map/ppermute | solution.py:241
  23.2 0.0 copy-start.8
  23.2 11.7 %all-to-all-done.states_ref = f32[128,1,640]{2,1,0:T(1,128)S(1)} async-done(((f32[128,1,640]{2,1,0:T(1,128)}), f32[128,1,640]{2,1,0:T(1,128)S(1)}, u32[]{:S(2)}, u32[]{:S(2)}) %all-to-all-start) | async-done | bytes 327712 | tf_op jit(solution)/shard_map/all_to_all | solution.py:240
  34.9 0.0 copy-done.8
  34.9 3.2 %carry.1 = (bf16[128,4,128]{2,1,0:T(4,128)(2,1)}, s32[1]{0:T(128)}) custom-call(s32[1]{0:T(128)} %bitcast.1.own_ref, s32[8]{0:T(128)S(1)} %copy-done.8, f32[128,1,640]{2,1,0:T(1,128)S(1)} %all-to-all-done.states_ref), custom_call_target="tpu_custom_call" | custom-call | tf_op jit(solution)/shard_map/carry/pallas_call | solution.py:264
  38.1 0.0 copy-start.3
  38.2 8.3 %all-to-all-start.1 = ((bf16[128,4,128]{2,1,0:T(4,128)(2,1)}), bf16[128,4,128]{2,1,0:T(4,128)(2,1)S(1)}, u32[]{:S(2)}, u32[]{:S(2)}) async-start(bf16[128,4,128]{2,1,0:T(4,128)(2,1)} %get-tuple-element.18), calls=%async_computation.1 | async-start | bytes 262144 | tf_op jit(solution)/shard_map/all_to_all | solution.py:265
  46.4 0.0 collective-permute-done
  46.5 0.0 copy-start.7
  46.5 0.0 copy-start
  46.5 0.0 copy-start.1
  46.5 0.0 copy-start.9
  46.5 0.0 copy-start.10
  46.6 4.8 %collective-permute-start.3 = (bf16[2,256,256]{2,1,0:T(8,128)(2,1)S(1)}, bf16[2,256,256]{2,1,0:T(8,128)(2,1)S(1)}, u32[]{:S(2)}, u32[]{:S(2)}) collective-permute-start(bf16[2,256,256]{2,1,0:T(8,128)(2,1)S(1)} %pad_maximum_fusion.refs_0_), channel_id=1, source_target_pairs={{0,3},{1,0},{2,1},{3,2},{4,7},{5,4},{6,5},{7,6},{8,11},{9,8},{10,9... | collective-permute-start | bytes 786440 | tf_op jit(solution)/shard_map/ppermute | solution.py:245
  51.4 2.7 %collective-permute-start.2 = (bf16[2,256,256]{2,1,0:T(8,128)(2,1)S(1)}, bf16[2,256,256]{2,1,0:T(8,128)(2,1)S(1)}, u32[]{:S(2)}, u32[]{:S(2)}) collective-permute-start(bf16[2,256,256]{2,1,0:T(8,128)(2,1)S(1)} %pad_maximum_fusion.refs_0_), channel_id=1, source_target_pairs={{0,2},{1,3},{2,0},{3,1},{4,6},{5,7},{6,4},{7,5},{8,10},{9,11},{10,... | collective-permute-start | bytes 786440 | tf_op jit(solution)/shard_map/ppermute | solution.py:245
  54.1 2.8 %collective-permute-start.1 = (bf16[2,256,256]{2,1,0:T(8,128)(2,1)S(1)}, bf16[2,256,256]{2,1,0:T(8,128)(2,1)S(1)}, u32[]{:S(2)}, u32[]{:S(2)}) collective-permute-start(bf16[2,256,256]{2,1,0:T(8,128)(2,1)S(1)} %pad_maximum_fusion.refs_0_), channel_id=1, source_target_pairs={{0,1},{1,2},{2,3},{3,0},{4,5},{5,6},{6,7},{7,4},{8,9},{9,10},{10,1... | collective-permute-start | bytes 786440 | tf_op jit(solution)/shard_map/ppermute | solution.py:245
  56.9 0.0 copy-done.3
  56.9 0.0 copy-done.7
  56.9 0.0 copy-done
  56.9 0.0 copy-done.1
  56.9 0.0 copy-done.9
  56.9 0.0 copy-done.10
  56.9 1.2 %inner.1 = (f32[256,512]{1,0:T(8,128)S(1)}, bf16[256,512]{1,0:T(8,128)(2,1)S(1)}, f32[8,512]{1,0:T(8,128)S(1)}) custom-call(bf16[256,512]{1,0:T(8,128)(2,1)S(1)} %copy-done.3, bf16[256,512]{1,0:T(8,128)(2,1)S(1)} %copy-done, bf16[256,512]{1,0:T(8,128)(2,1)S(1)} %copy-done.1, f32[1,512]{1,0:T(1,128)S(1)} %bitcast.20, s32[8]{0:T(128)S(1)} %copy-done.9, ...), custom_call_target="tpu_custom_call" | custom-call | tf_op jit(solution)/shard_map/inner/pallas_call | solution.py:246
  58.2 0.0 all-to-all-done.1.carried_ref
  58.2 2.0 %attention.1 = (bf16[256,512]{1,0:T(8,128)(2,1)}, bf16[272,512]{1,0:T(8,128)(2,1)S(1)}) custom-call(bf16[256,512]{1,0:T(8,128)(2,1)S(1)} %get-tuple-element.16.first_ref, f32[256,512]{1,0:T(8,128)S(1)} %get-tuple-element.17.inner_ref, bf16[128,4,128]{2,1,0:T(4,128)(2,1)S(1)} %all-to-all-done.1.carried_ref, f32[8,512]{1,0:T(8,128)S(1)} %get-tuple-element.19.lines_ref, ...), custom_call_target="tpu_custom_call" | custom-call | tf_op jit(solution)/shard_map/attention/pallas_call | solution.py:266
  60.1 2.2 %all-gather = bf16[544,512]{1,0:T(8,128)(2,1)S(1)} all-gather(bf16[272,512]{1,0:T(8,128)(2,1)S(1)} %get-tuple-element.22), channel_id=2, replica_groups=mesh['chip'=64,'core'=2,'group'=4] {'core'}, dimensions={0}, use_global_device_ids=true | all-gather | bytes 835584 | tf_op jit(solution)/shard_map/all_gather | solution.py:273
  62.3 0.5 collective-permute-done.3.refs_3_
  62.8 1.1 %collective-permute-done.2.refs_2_ = bf16[2,256,256]{2,1,0:T(8,128)(2,1)S(1)} collective-permute-done((bf16[2,256,256]{2,1,0:T(8,128)(2,1)S(1)}, bf16[2,256,256]{2,1,0:T(8,128)(2,1)S(1)}, u32[]{:S(2)}, u32[]{:S(2)}) %collective-permute-start.2) | collective-permute-done | bytes 262176 | tf_op jit(solution)/shard_map/ppermute | solution.py:245
  64.0 4.4 %collective-permute-done.1.refs_1_ = bf16[2,256,256]{2,1,0:T(8,128)(2,1)S(1)} collective-permute-done((bf16[2,256,256]{2,1,0:T(8,128)(2,1)S(1)}, bf16[2,256,256]{2,1,0:T(8,128)(2,1)S(1)}, u32[]{:S(2)}, u32[]{:S(2)}) %collective-permute-start.1) | collective-permute-done | bytes 262176 | tf_op jit(solution)/shard_map/ppermute | solution.py:245
  68.4 1.3 %gradient.1 = bf16[1024,512]{1,0:T(8,128)(2,1)S(1)} custom-call(s32[2]{0:T(128)S(1)} %pad_add_fusion.refs_1_.place_ref, bf16[2,272,512]{2,1,0:T(8,128)(2,1)S(1)} %bitcast.15, bf16[2,256,256]{2,1,0:T(8,128)(2,1)S(1)} %pad_maximum_fusion.refs_0_, bf16[2,256,256]{2,1,0:T(8,128)(2,1)S(1)} %collective-permute-done.1.refs_1_, ...), custom_call_target="tpu_custom_call" | custom-call | tf_op jit(solution)/shard_map/gradient/pallas_call | solution.py:274
  69.7 0.0 copy-start.4
  69.7 0.0 copy-start.5
  69.7 0.0 copy-start.6
  69.7 43.3 %all_to_all.15.parts_ref = bf16[64,16,512]{2,1,0:T(8,128)(2,1)S(1)} all-to-all(bf16[64,16,512]{2,1,0:T(8,128)(2,1)S(1)} %bitcast.14), channel_id=1, replica_groups=mesh['chip'=64,'core'=2,'group'=4] {'chip'}, dimensions={0} | all-to-all | bytes 2097152 | tf_op jit(solution)/shard_map/all_to_all | solution.py:281
  113.0 0.0 copy-done.4
  113.0 0.0 copy-done.5
  113.0 0.0 copy-done.6
  113.0 0.9 update.1
  (1 shorter events, 0.0 us)
Async XLA Ops:
  2.9 17.6 %copy-start.2 = (bf16[256,512]{1,0:T(8,128)(2,1)S(1)}, bf16[256,512]{1,0:T(8,128)(2,1)}, u32[]{:S(2)}) copy-start(bf16[256,512]{1,0:T(8,128)(2,1)} %refs_0_.1) | copy-start | bytes 786436
  2.9 32.0 %all-to-all-start = ((f32[128,1,640]{2,1,0:T(1,128)}), f32[128,1,640]{2,1,0:T(1,128)S(1)}, u32[]{:S(2)}, u32[]{:S(2)}) async-start(f32[128,1,640]{2,1,0:T(1,128)} %state.1), calls=%async_computation | async-start | bytes 655360 | tf_op jit(solution)/shard_map/all_to_all | solution.py:240
  21.2 25.3 %collective-permute-start = (bf16[256,256]{1,0:T(8,128)(2,1)S(1)}, bf16[256,256]{1,0:T(8,128)(2,1)S(1)}, u32[]{:S(2)}, u32[]{:S(2)}) collective-permute-start(bf16[256,256]{1,0:T(8,128)(2,1)S(1)} %get-tuple-element.24), channel_id=1, source_target_pairs={{0,4},{4,0},{1,5},{5,1},{2,6},{6,2},{3,7},{7,3},{8,12},{12,8},{9,1... | collective-permute-start | bytes 393224 | tf_op jit(solution)/shard_map/ppermute | solution.py:241
  23.2 11.7 %copy-start.8 = (s32[8]{0:T(128)S(1)}, s32[8]{0:T(128)}, u32[]{:S(2)}) copy-start(s32[8]{0:T(128)} %weights_ref.3) | copy-start | bytes 100
  38.1 18.7 %copy-start.3 = (bf16[256,512]{1,0:T(8,128)(2,1)S(1)}, bf16[256,512]{1,0:T(8,128)(2,1)}, u32[]{:S(2)}) copy-start(bf16[256,512]{1,0:T(8,128)(2,1)} %query_ref.1) | copy-start | bytes 786436
  38.2 20.0 %all-to-all-start.1 = ((bf16[128,4,128]{2,1,0:T(4,128)(2,1)}), bf16[128,4,128]{2,1,0:T(4,128)(2,1)S(1)}, u32[]{:S(2)}, u32[]{:S(2)}) async-start(bf16[128,4,128]{2,1,0:T(4,128)(2,1)} %get-tuple-element.18), calls=%async_computation.1 | async-start | bytes 262144 | tf_op jit(solution)/shard_map/all_to_all | solution.py:265
  46.5 10.4 %copy-start.7 = (f32[512]{0:T(512)S(1)}, f32[512]{0:T(512)}, u32[]{:S(2)}) copy-start(f32[512]{0:T(512)} %param.14) | copy-start | bytes 6148
  46.5 10.4 %copy-start = (bf16[256,512]{1,0:T(8,128)(2,1)S(1)}, bf16[256,512]{1,0:T(8,128)(2,1)}, u32[]{:S(2)}) copy-start(bf16[256,512]{1,0:T(8,128)(2,1)} %key_hbm.1) | copy-start | bytes 786436
  46.5 10.4 %copy-start.1 = (bf16[256,512]{1,0:T(8,128)(2,1)S(1)}, bf16[256,512]{1,0:T(8,128)(2,1)}, u32[]{:S(2)}) copy-start(bf16[256,512]{1,0:T(8,128)(2,1)} %value_hbm.1) | copy-start | bytes 786436
  46.5 10.4 %copy-start.9 = (s32[8]{0:T(128)S(1)}, s32[8]{0:T(128)}, u32[]{:S(2)}) copy-start(s32[8]{0:T(128)} %starts_hbm.1) | copy-start | bytes 100
  46.5 10.4 %copy-start.10 = (s32[8]{0:T(128)S(1)}, s32[8]{0:T(128)}, u32[]{:S(2)}) copy-start(s32[8]{0:T(128)} %domains_hbm.1) | copy-start | bytes 100
  46.6 16.3 %collective-permute-start.3 = (bf16[2,256,256]{2,1,0:T(8,128)(2,1)S(1)}, bf16[2,256,256]{2,1,0:T(8,128)(2,1)S(1)}, u32[]{:S(2)}, u32[]{:S(2)}) collective-permute-start(bf16[2,256,256]{2,1,0:T(8,128)(2,1)S(1)} %pad_maximum_fusion.refs_0_), channel_id=1, source_target_pairs={{0,3},{1,0},{2,1},{3,2},{4,7},{5,4},{6,5},{7,6},{8,11},{9,8},{10,9... | collective-permute-start | bytes 786440 | tf_op jit(solution)/shard_map/ppermute | solution.py:245
  51.4 12.6 %collective-permute-start.2 = (bf16[2,256,256]{2,1,0:T(8,128)(2,1)S(1)}, bf16[2,256,256]{2,1,0:T(8,128)(2,1)S(1)}, u32[]{:S(2)}, u32[]{:S(2)}) collective-permute-start(bf16[2,256,256]{2,1,0:T(8,128)(2,1)S(1)} %pad_maximum_fusion.refs_0_), channel_id=1, source_target_pairs={{0,2},{1,3},{2,0},{3,1},{4,6},{5,7},{6,4},{7,5},{8,10},{9,11},{10,... | collective-permute-start | bytes 786440 | tf_op jit(solution)/shard_map/ppermute | solution.py:245
  54.1 14.4 %collective-permute-start.1 = (bf16[2,256,256]{2,1,0:T(8,128)(2,1)S(1)}, bf16[2,256,256]{2,1,0:T(8,128)(2,1)S(1)}, u32[]{:S(2)}, u32[]{:S(2)}) collective-permute-start(bf16[2,256,256]{2,1,0:T(8,128)(2,1)S(1)} %pad_maximum_fusion.refs_0_), channel_id=1, source_target_pairs={{0,1},{1,2},{2,3},{3,0},{4,5},{5,6},{6,7},{7,4},{8,9},{9,10},{10,1... | collective-permute-start | bytes 786440 | tf_op jit(solution)/shard_map/ppermute | solution.py:245
  69.7 43.3 %copy-start.4 = (f32[512,16]{0,1:T(8,128)S(1)}, f32[512,16]{0,1:T(8,128)}, u32[]{:S(2)}) copy-start(f32[512,16]{0,1:T(8,128)} %param.19) | copy-start | bytes 98308
  69.7 43.3 %copy-start.5 = (f32[512,16]{0,1:T(8,128)S(1)}, f32[512,16]{0,1:T(8,128)}, u32[]{:S(2)}) copy-start(f32[512,16]{0,1:T(8,128)} %param.20) | copy-start | bytes 98308
  69.7 43.3 %copy-start.6 = (f32[512,16]{0,1:T(8,128)S(1)}, f32[512,16]{0,1:T(8,128)}, u32[]{:S(2)}) copy-start(f32[512,16]{0,1:T(8,128)} %param.21) | copy-start | bytes 98308

commit v4 on v3

--- a/solution.py
+++ b/solution.py
@@ -1,3 +1,5 @@
+import math
+
 import jax
 import jax.numpy as jnp
 from jax import lax
@@ -75,7 +77,7 @@
     )
 
 
-def carry_kernel(own_ref, weights_ref, states_ref, carried_ref, weight_ref, total_ref):
+def carry_kernel(weights_ref, states_ref, carried_ref, weight_ref, total_ref):
     total, blocks = states_ref.shape[0], carried_ref.shape[0]
     rows, heads = total // blocks, carried_ref.shape[1] // (total // blocks)
     width = heads * HEAD_DIM
@@ -90,26 +92,28 @@
     )
     joined = jnp.where((there < here) & (there >= latest), 1.0, 0.0).astype(bf16)
     for row in range(rows):
-        state = states_ref[row::rows, 0, :width] if rows > 1 else states_ref[:, 0, :width]
-        high = state.astype(bf16)
-        rest = state - high.astype(f32)
-        middle = rest.astype(bf16)
-        low = (rest - middle.astype(f32)).astype(bf16)
-        summed = dot(joined, high, ((1,), (0,)))
-        summed = summed + dot(joined, middle, ((1,), (0,)))
-        summed = summed + dot(joined, low, ((1,), (0,)))
         for head in range(heads):
             cols = slice(head * HEAD_DIM, (head + 1) * HEAD_DIM)
-            total_ref[:, row * heads + head, :] = summed[:, cols]
+            state = states_ref[row::rows, 0, cols] if rows > 1 else states_ref[:, 0, cols]
+            high = state.astype(bf16)
+            rest = state - high.astype(f32)
+            middle = rest.astype(bf16)
+            low = (rest - middle.astype(f32)).astype(bf16)
+            summed = dot(joined, high, ((1,), (0,)))
+            summed = summed + dot(joined, middle, ((1,), (0,)))
+            summed = summed + dot(joined, low, ((1,), (0,)))
+            total_ref[:, row * heads + head, :] = summed
     carried_ref[...] = total_ref[...].astype(bf16)
+    own = lax.axis_index("chip") * 2 + lax.axis_index("core")
     block_ids = iota((blocks, 1), 0)
-    before = (flag_col > 0.0) & (block_ids < own_ref[0])
-    last_block = jnp.max(jnp.where(before, block_ids, -1))
-    domain = jnp.sum(jnp.where(block_ids == last_block, domain_col, 0.0)).astype(i32)
-    weight = jnp.int32(0)
-    for which in range(weights_ref.shape[0]):
-        weight = jnp.where(domain == which, weights_ref[which], weight)
-    weight_ref[0] = weight
+    before = (flag_col > 0.0) & (block_ids < own)
+    last_block = jnp.max(jnp.where(before, block_ids, -1), axis=0, keepdims=True)
+    domain = jnp.sum(jnp.where(block_ids == last_block, domain_col, 0.0), axis=0, keepdims=True)
+    slot = iota(weights_ref.shape, 1).astype(f32)
+    weight = jnp.sum(
+        jnp.where(slot == domain, weights_ref[...].astype(f32), 0.0), axis=1, keepdims=True
+    )
+    weight_ref[...] = jnp.broadcast_to(weight, weight_ref.shape)
 
 
 def inner_kernel(
@@ -141,7 +145,7 @@
 
 
 def attention_kernel(
-    first_ref, inner_ref, carried_ref, lines_ref, weight_in_ref, out_ref, shared_ref, state_ref
+    first_ref, inner_ref, carried_ref, lines_ref, weight_in_ref, shared_ref, state_ref
 ):
     row_count, width = first_ref.shape
     state_ref[...] = carried_ref[...].astype(f32)
@@ -150,11 +154,9 @@
         state = state_ref[:, head, :].astype(bf16)
         raw = inner_ref[:, cols] + dot(first_ref[:, cols], state, ((1,), (0,)))
         scale = lax.rsqrt(jnp.mean(raw * raw, axis=1, keepdims=True) + 1e-05)
-        normed = (raw * scale * lines_ref[0:1, cols]).astype(bf16)
-        out_ref[:, cols] = normed
-        shared_ref[:row_count, cols] = normed
+        shared_ref[:row_count, cols] = (raw * scale * lines_ref[0:1, cols]).astype(bf16)
     line = lines_ref[1:2, :]
-    line = jnp.where(line == 0.0, weight_in_ref[0].astype(f32), line)
+    line = jnp.where(line == 0.0, weight_in_ref[0:1, 0:1], line)
     shared_ref[row_count:, :] = jnp.broadcast_to(line, (16, width)).astype(bf16)
 
 
@@ -167,20 +169,35 @@
             out_ref[pair * owned : (pair + 1) * owned] = turned_ref[pl.ds(start, owned), :]
 
 
-def gradient_kernel(place_ref, shared_ref, *refs):
-    cotangent_refs, out_ref = refs[:-1], refs[-1]
+def gradient_kernel(shared_ref, *refs, owned, side):
+    cotangent_refs, (out_ref, attention_ref, sent) = refs[:-3], refs[-3:]
     groups = len(cotangent_refs)
     _, cols, row_count = cotangent_refs[0].shape
+    core, own_group = lax.axis_index("core"), lax.axis_index("group")
+    save = pltpu.make_async_copy(shared_ref.at[core, :row_count], attention_ref, sent)
+    save.start()
     for shift, cotangent_ref in enumerate(cotangent_refs):
         total = None
-        for side in range(2):
-            core = jnp.where(side == 0, place_ref[0], 1 - place_ref[0])
-            weight = shared_ref[core, row_count : row_count + 1, :row_count].astype(f32)
-            weighted = (cotangent_ref[side].astype(f32) * weight).astype(bf16)
-            part = dot(weighted, shared_ref[core, :row_count, :], ((1,), (0,)))
+        for which in (core, 1 - core):
+            near = 0 if total is None else 1
+            weight = shared_ref[which, row_count : row_count + 1, :row_count].astype(f32)
+            weighted = (cotangent_ref[near].astype(f32) * weight).astype(bf16)
+            part = dot(weighted, shared_ref[which, :row_count, :], ((1,), (0,)))
             total = part if total is None else total + part
-        group = lax.rem(place_ref[1] - shift + groups, groups)
-        out_ref[pl.ds(pl.multiple_of(group * cols, cols), cols), :] = total.astype(bf16)
+        total = total.astype(bf16)
+        group = lax.rem(own_group - shift + groups, groups)
+        for block in range(cols // owned):
+            owner = group * (cols // owned) + block
+            down, along = owner // side, lax.rem(owner, side)
+            place = jnp.where(core == 0, along * side + down, owner)
+            out_ref[pl.ds(pl.multiple_of(place * owned, owned), owned), :] = total[
+                block * owned : (block + 1) * owned
+            ]
+    save.wait()
+
+
+def sum_kernel(parts_ref, out_ref):
+    out_ref[...] = jnp.sum(parts_ref[...].astype(f32), axis=0).astype(bf16)
 
 
 def update_kernel(
@@ -212,10 +229,10 @@
     row_count, width = queries.shape
     owned = weight.shape[1]
     rows, heads = HEAD_DIM // blocks, width // HEAD_DIM
-    own_block = (lax.axis_index("chip") * 2 + lax.axis_index("core")).reshape(1).astype(i32)
     V, S = VMEM_SPEC, SMEM_SPEC
 
-    place = jnp.stack([lax.axis_index("core"), lax.axis_index("group")]).astype(i32)
+    core, group = lax.axis_index("core"), lax.axis_index("group")
+    place = jnp.stack([core, group]).astype(i32)
     own_half, other_half = pl.pallas_call(
         lambda *refs: turn_kernel(*refs, owned=owned),
         out_shape=(shape((width // 2, row_count), bf16),) * 2,
@@ -225,7 +242,7 @@
     )(cotangent, place)
     states = pl.pallas_call(
         state_kernel,
-        out_shape=shape((HEAD_DIM, 1, width + LANES), f32),
+        out_shape=pltpu.VMEM((HEAD_DIM, 1, width + LANES), f32),
         in_specs=[HBM_SPEC] * 4, out_specs=V,
         scratch_shapes=[
             pltpu.VMEM(key_rows.shape, bf16), pltpu.VMEM(value_rows.shape, bf16),
@@ -256,29 +273,50 @@
     )
     carry_call = pl.pallas_call(
         carry_kernel,
-        out_shape=(shape((blocks, rows * heads, HEAD_DIM), bf16), shape((1,), i32)),
-        in_specs=[S, S, V], out_specs=(V, S),
+        out_shape=(
+            pltpu.VMEM((blocks, rows * heads, HEAD_DIM), bf16), shape((8, LANES), f32),
+        ),
+        in_specs=[V, V], out_specs=(V, V),
         scratch_shapes=[pltpu.VMEM((blocks, rows * heads, HEAD_DIM), f32)],
         compiler_params=SMALL, name="carry",
     )
-    carried, weight_in = carry_call(own_block, domain_weights, states)
+    carried, weight_in = carry_call(domain_weights.reshape(1, -1), states)
     carried = lax.all_to_all(carried, ("chip", "core"), 0, 0, tiled=True)
-    attention, shared = pl.pallas_call(
+    shared = pl.pallas_call(
         attention_kernel,
-        out_shape=(shape((row_count, width), bf16), shape((row_count + 16, width), bf16)),
-        in_specs=[V, V, V, V, S], out_specs=(V, V),
+        out_shape=shape((row_count + 16, width), bf16),
+        in_specs=[V] * 5, out_specs=V,
         scratch_shapes=[pltpu.VMEM((HEAD_DIM, heads, HEAD_DIM), f32)],
         compiler_params=SMALL, name="attention",
     )(first, inner, carried.reshape(HEAD_DIM, heads, HEAD_DIM), lines, weight_in)
     shared = lax.all_gather(shared, "core", axis=0, tiled=False)
+    side = math.isqrt(chips)
+    partial, attention = pl.pallas_call(
+        lambda *refs: gradient_kernel(*refs, owned=owned, side=side),
+        out_shape=(
+            shape((groups * width // 2, width), bf16), shape((row_count, width), bf16)
+        ),
+        in_specs=[V] * (1 + groups), out_specs=(V, HBM_SPEC),
+        scratch_shapes=[pltpu.SemaphoreType.DMA],
+        compiler_params=SMALL, name="gradient",
+    )(shared, *turned)
+    lines_of = [
+        [[(y * side + z) * 2 + c for z in range(side)] for y in range(side)] for c in range(2)
+    ]
+    rows_of = [[list(line) for line in zip(*lines)] for lines in lines_of]
+    partial = lax.all_to_all(
+        partial.reshape(side, side * owned, width), ("chip", "core"), 0, 0, tiled=True,
+        axis_index_groups=lines_of[0] + rows_of[1],
+    )
     partial = pl.pallas_call(
-        gradient_kernel,
-        out_shape=shape((groups * width // 2, width), bf16),
-        in_specs=[S] + [V] * (1 + groups), out_specs=V,
-        compiler_params=SMALL, name="gradient",
-    )(place, shared, *turned)
-    partial = partial.reshape(chips, owned, width)
-    partial = lax.all_to_all(partial, "chip", 0, 0, tiled=True)
+        sum_kernel,
+        out_shape=shape((side * owned, width), bf16),
+        in_specs=[V], out_specs=V, compiler_params=SMALL, name="sum",
+    )(partial)
+    partial = lax.all_to_all(
+        partial.reshape(side, owned, width), ("chip", "core"), 0, 0, tiled=True,
+        axis_index_groups=rows_of[0] + lines_of[1],
+    )
     new_weight, new_first, new_second = pl.pallas_call(
         update_kernel,
         out_shape=(shape((owned, width), f32),) * 3,

time: 114 us -> 111 us (0.974)
  the two profiles are of different devices: /device:TPU:16 before, /device:TPU:8 now
where the time goes in v4:
time: 111 us; the launch traced here: 110 us
  blocking collectives  42.7 us (38%)
  starting transfers between devices  36.5 us (33%)
  waiting for transfers between devices  20.7 us (19%)
  Pallas kernels  9.3 us (8%)
    all_to_all x1, blocking collectives, on_device(): lax.all_to_all(partial.reshape(side, side * owned, width), ('chip', 'core...  25.4 us
    all_to_all x1, starting transfers between devices, on_device(): states = lax.all_to_all(states, ('chip', 'core'), 0, 0, tiled=True)  17.5 us
    all_to_all x1, blocking collectives, on_device(): lax.all_to_all(partial.reshape(side, owned, width), ('chip', 'core'), 0,...  15.1 us
    all_to_all x1, waiting for transfers between devices, on_device(): states = lax.all_to_all(states, ('chip', 'core'), 0, 0, tiled=True)  13.3 us
    ppermute x3, starting transfers between devices, on_device(): lax.ppermute(halves, 'group', [(g, (g + k) % groups) for g in range(group...  10.3 us
    ppermute x3, waiting for transfers between devices, on_device(): lax.ppermute(halves, 'group', [(g, (g + k) % groups) for g in range(group...  7.18 us
    all_to_all x1, starting transfers between devices, on_device(): carried = lax.all_to_all(carried, ('chip', 'core'), 0, 0, tiled=True)  6.68 us
    pallas_call x1, Pallas kernels, on_device(): carried, weight_in = carry_call(domain_weights.reshape(1, -1), states)  2.35 us
  transfers between devices with their start and end apart: 6, of which 5 were waited for; matrix products, arithmetic and copies ran while one was open for 0% of the time, Pallas kernels for 4%

profile of v4, /device:TPU:8, one launch (start us, length us, event | category | flops | bytes accessed | tf_op | source)
XLA Modules:
  0.0 110.3 jit_solution(956917772202624800)
XLA Ops:
  0.6 2.3 %state.1 = f32[128,1,640]{2,1,0:T(1,128)} custom-call(bf16[256,512]{1,0:T(8,128)(2,1)} %key_hbm.1, bf16[256,512]{1,0:T(8,128)(2,1)} %value_hbm.1, s32[8]{0:T(128)} %starts_hbm.1, s32[8]{0:T(128)} %domains_hbm.1), custom_call_target="tpu_custom_call" | custom-call | tf_op jit(solution)/shard_map/state/pallas_call | solution.py:243
  2.9 0.0 copy-start.2
  2.9 17.5 %all-to-all-start = ((f32[128,1,640]{2,1,0:T(1,128)}), f32[128,1,640]{2,1,0:T(1,128)S(1)}, u32[]{:S(2)}, u32[]{:S(2)}) async-start(f32[128,1,640]{2,1,0:T(1,128)} %state.1), calls=%async_computation | async-start | bytes 655360 | tf_op jit(solution)/shard_map/all_to_all | solution.py:257
  20.4 0.1 pad_add_fusion.refs_1_
  20.5 0.0 copy-done.2
  20.5 0.7 turn.1
  21.2 0.0 copy-start.8
  21.2 2.0 %collective-permute-start = (bf16[256,256]{1,0:T(8,128)(2,1)S(1)}, bf16[256,256]{1,0:T(8,128)(2,1)S(1)}, u32[]{:S(2)}, u32[]{:S(2)}) collective-permute-start(bf16[256,256]{1,0:T(8,128)(2,1)S(1)} %get-tuple-element.22), channel_id=1, source_target_pairs={{0,4},{4,0},{1,5},{5,1},{2,6},{6,2},{3,7},{7,3},{8,12},{12,8},{9,1... | collective-permute-start | bytes 393224 | tf_op jit(solution)/shard_map/ppermute | solution.py:258
  23.2 13.3 %all-to-all-done.states_ref = f32[128,1,640]{2,1,0:T(1,128)S(1)} async-done(((f32[128,1,640]{2,1,0:T(1,128)}), f32[128,1,640]{2,1,0:T(1,128)S(1)}, u32[]{:S(2)}, u32[]{:S(2)}) %all-to-all-start) | async-done | bytes 327712 | tf_op jit(solution)/shard_map/all_to_all | solution.py:257
  36.5 0.0 copy-done.8
  36.5 2.3 %carry.1 = (bf16[128,4,128]{2,1,0:T(4,128)(2,1)}, f32[8,128]{1,0:T(8,128)S(1)}) custom-call(s32[1,8]{1,0:T(1,128)S(1)} %bitcast.23, f32[128,1,640]{2,1,0:T(1,128)S(1)} %all-to-all-done.states_ref), custom_call_target="tpu_custom_call" | custom-call | tf_op jit(solution)/shard_map/carry/pallas_call | solution.py:283
  38.9 0.0 copy-start.3
  38.9 6.7 %all-to-all-start.1 = ((bf16[128,4,128]{2,1,0:T(4,128)(2,1)}), bf16[128,4,128]{2,1,0:T(4,128)(2,1)S(1)}, u32[]{:S(2)}, u32[]{:S(2)}) async-start(bf16[128,4,128]{2,1,0:T(4,128)(2,1)} %get-tuple-element.18), calls=%async_computation.1 | async-start | bytes 262144 | tf_op jit(solution)/shard_map/all_to_all | solution.py:284
  45.6 0.0 collective-permute-done
  45.6 0.0 copy-start.7
  45.6 0.0 copy-start
  45.6 0.0 copy-start.1
  45.7 0.0 copy-start.9
  45.7 0.0 copy-start.10
  45.7 4.8 %collective-permute-start.3 = (bf16[2,256,256]{2,1,0:T(8,128)(2,1)S(1)}, bf16[2,256,256]{2,1,0:T(8,128)(2,1)S(1)}, u32[]{:S(2)}, u32[]{:S(2)}) collective-permute-start(bf16[2,256,256]{2,1,0:T(8,128)(2,1)S(1)} %pad_maximum_fusion.refs_1_), channel_id=1, source_target_pairs={{0,3},{1,0},{2,1},{3,2},{4,7},{5,4},{6,5},{7,6},{8,11},{9,8},{10,9... | collective-permute-start | bytes 786440 | tf_op jit(solution)/shard_map/ppermute | solution.py:262
  50.5 2.7 %collective-permute-start.2 = (bf16[2,256,256]{2,1,0:T(8,128)(2,1)S(1)}, bf16[2,256,256]{2,1,0:T(8,128)(2,1)S(1)}, u32[]{:S(2)}, u32[]{:S(2)}) collective-permute-start(bf16[2,256,256]{2,1,0:T(8,128)(2,1)S(1)} %pad_maximum_fusion.refs_1_), channel_id=1, source_target_pairs={{0,2},{1,3},{2,0},{3,1},{4,6},{5,7},{6,4},{7,5},{8,10},{9,11},{10,... | collective-permute-start | bytes 786440 | tf_op jit(solution)/shard_map/ppermute | solution.py:262
  53.2 2.8 %collective-permute-start.1 = (bf16[2,256,256]{2,1,0:T(8,128)(2,1)S(1)}, bf16[2,256,256]{2,1,0:T(8,128)(2,1)S(1)}, u32[]{:S(2)}, u32[]{:S(2)}) collective-permute-start(bf16[2,256,256]{2,1,0:T(8,128)(2,1)S(1)} %pad_maximum_fusion.refs_1_), channel_id=1, source_target_pairs={{0,1},{1,2},{2,3},{3,0},{4,5},{5,6},{6,7},{7,4},{8,9},{9,10},{10,1... | collective-permute-start | bytes 786440 | tf_op jit(solution)/shard_map/ppermute | solution.py:262
  56.0 0.0 copy-done.3
  56.0 0.0 copy-done.7
  56.0 0.0 copy-done
  56.0 0.0 copy-done.1
  56.1 0.0 copy-done.9
  56.1 0.0 copy-done.10
  56.1 1.2 %inner.1 = (f32[256,512]{1,0:T(8,128)S(1)}, bf16[256,512]{1,0:T(8,128)(2,1)S(1)}, f32[8,512]{1,0:T(8,128)S(1)}) custom-call(bf16[256,512]{1,0:T(8,128)(2,1)S(1)} %copy-done.3, bf16[256,512]{1,0:T(8,128)(2,1)S(1)} %copy-done, bf16[256,512]{1,0:T(8,128)(2,1)S(1)} %copy-done.1, f32[1,512]{1,0:T(1,128)S(1)} %bitcast.22, s32[8]{0:T(128)S(1)} %copy-done.9, ...), custom_call_target="tpu_custom_call" | custom-call | tf_op jit(solution)/shard_map/inner/pallas_call | solution.py:263
  57.3 0.3 all-to-all-done.1.carried_ref
  57.6 0.6 attention.1
  58.2 2.2 %all-gather = bf16[544,512]{1,0:T(8,128)(2,1)S(1)} all-gather(bf16[272,512]{1,0:T(8,128)(2,1)S(1)} %attention.1), channel_id=2, replica_groups=mesh['chip'=64,'core'=2,'group'=4] {'core'}, dimensions={0}, use_global_device_ids=true | all-gather | bytes 835584 | tf_op jit(solution)/shard_map/all_gather | solution.py:292
  60.4 1.6 %collective-permute-done.3.refs_4_ = bf16[2,256,256]{2,1,0:T(8,128)(2,1)S(1)} collective-permute-done((bf16[2,256,256]{2,1,0:T(8,128)(2,1)S(1)}, bf16[2,256,256]{2,1,0:T(8,128)(2,1)S(1)}, u32[]{:S(2)}, u32[]{:S(2)}) %collective-permute-start.3) | collective-permute-done | bytes 262176 | tf_op jit(solution)/shard_map/ppermute | solution.py:262
  62.0 1.1 %collective-permute-done.2.refs_3_ = bf16[2,256,256]{2,1,0:T(8,128)(2,1)S(1)} collective-permute-done((bf16[2,256,256]{2,1,0:T(8,128)(2,1)S(1)}, bf16[2,256,256]{2,1,0:T(8,128)(2,1)S(1)}, u32[]{:S(2)}, u32[]{:S(2)}) %collective-permute-start.2) | collective-permute-done | bytes 262176 | tf_op jit(solution)/shard_map/ppermute | solution.py:262
  63.1 4.4 %collective-permute-done.1.refs_2_ = bf16[2,256,256]{2,1,0:T(8,128)(2,1)S(1)} collective-permute-done((bf16[2,256,256]{2,1,0:T(8,128)(2,1)S(1)}, bf16[2,256,256]{2,1,0:T(8,128)(2,1)S(1)}, u32[]{:S(2)}, u32[]{:S(2)}) %collective-permute-start.1) | collective-permute-done | bytes 262176 | tf_op jit(solution)/shard_map/ppermute | solution.py:262
  67.6 1.4 %gradient.1 = (bf16[1024,512]{1,0:T(8,128)(2,1)S(1)}, bf16[256,512]{1,0:T(8,128)(2,1)}) custom-call(bf16[2,272,512]{2,1,0:T(8,128)(2,1)S(1)} %bitcast.15, bf16[2,256,256]{2,1,0:T(8,128)(2,1)S(1)} %pad_maximum_fusion.refs_1_, bf16[2,256,256]{2,1,0:T(8,128)(2,1)S(1)} %collective-permute-done.1.refs_2_, ...), custom_call_target="tpu_custom_call" | custom-call | tf_op jit(solution)/shard_map/gradient/pallas_call | solution.py:294
  69.0 25.4 %all_to_all.20.parts_ref = bf16[8,128,512]{2,1,0:T(8,128)(2,1)S(1)} all-to-all(bf16[8,128,512]{2,1,0:T(8,128)(2,1)S(1)} %bitcast.16), channel_id=1, replica_groups={{0,8,16,24,32,40,48,56},{64,72,80,88,96,104,112,120},{128,136,144,152,1..., dimensions={0} | all-to-all | bytes 2097152 | tf_op jit(solution)/shard_map/all_to_all | solution.py:307
  94.4 0.1 sum.1
  94.5 0.0 copy-start.4
  94.5 0.0 copy-start.5
  94.5 0.0 copy-start.6
  94.5 15.1 %all_to_all.21.parts_ref = bf16[8,16,512]{2,1,0:T(8,128)(2,1)S(1)} all-to-all(bf16[8,16,512]{2,1,0:T(8,128)(2,1)S(1)} %bitcast.17), channel_id=1, replica_groups={{0,64,128,192,256,320,384,448},{8,72,136,200,264,328,392,456},{16,80,14..., dimensions={0} | all-to-all | bytes 262144 | tf_op jit(solution)/shard_map/all_to_all | solution.py:316
  109.6 0.0 copy-done.4
  109.6 0.0 copy-done.5
  109.6 0.0 copy-done.6
  109.6 0.7 update.1
  (1 shorter events, 0.0 us)
Async XLA Ops:
  2.9 17.6 %copy-start.2 = (bf16[256,512]{1,0:T(8,128)(2,1)S(1)}, bf16[256,512]{1,0:T(8,128)(2,1)}, u32[]{:S(2)}) copy-start(bf16[256,512]{1,0:T(8,128)(2,1)} %refs_0_.1) | copy-start | bytes 786436
  2.9 33.6 %all-to-all-start = ((f32[128,1,640]{2,1,0:T(1,128)}), f32[128,1,640]{2,1,0:T(1,128)S(1)}, u32[]{:S(2)}, u32[]{:S(2)}) async-start(f32[128,1,640]{2,1,0:T(1,128)} %state.1), calls=%async_computation | async-start | bytes 655360 | tf_op jit(solution)/shard_map/all_to_all | solution.py:257
  21.2 15.3 %copy-start.8 = (s32[8]{0:T(128)S(1)}, s32[8]{0:T(128)}, u32[]{:S(2)}) copy-start(s32[8]{0:T(128)} %weights_ref.1) | copy-start | bytes 100
  21.2 24.4 %collective-permute-start = (bf16[256,256]{1,0:T(8,128)(2,1)S(1)}, bf16[256,256]{1,0:T(8,128)(2,1)S(1)}, u32[]{:S(2)}, u32[]{:S(2)}) collective-permute-start(bf16[256,256]{1,0:T(8,128)(2,1)S(1)} %get-tuple-element.22), channel_id=1, source_target_pairs={{0,4},{4,0},{1,5},{5,1},{2,6},{6,2},{3,7},{7,3},{8,12},{12,8},{9,1... | collective-permute-start | bytes 393224 | tf_op jit(solution)/shard_map/ppermute | solution.py:258
  38.9 17.1 %copy-start.3 = (bf16[256,512]{1,0:T(8,128)(2,1)S(1)}, bf16[256,512]{1,0:T(8,128)(2,1)}, u32[]{:S(2)}) copy-start(bf16[256,512]{1,0:T(8,128)(2,1)} %query_ref.1) | copy-start | bytes 786436
  38.9 18.7 %all-to-all-start.1 = ((bf16[128,4,128]{2,1,0:T(4,128)(2,1)}), bf16[128,4,128]{2,1,0:T(4,128)(2,1)S(1)}, u32[]{:S(2)}, u32[]{:S(2)}) async-start(bf16[128,4,128]{2,1,0:T(4,128)(2,1)} %get-tuple-element.18), calls=%async_computation.1 | async-start | bytes 262144 | tf_op jit(solution)/shard_map/all_to_all | solution.py:284
  45.6 10.4 %copy-start.7 = (f32[512]{0:T(512)S(1)}, f32[512]{0:T(512)}, u32[]{:S(2)}) copy-start(f32[512]{0:T(512)} %param.14) | copy-start | bytes 6148
  45.6 10.4 %copy-start = (bf16[256,512]{1,0:T(8,128)(2,1)S(1)}, bf16[256,512]{1,0:T(8,128)(2,1)}, u32[]{:S(2)}) copy-start(bf16[256,512]{1,0:T(8,128)(2,1)} %key_hbm.1) | copy-start | bytes 786436
  45.6 10.4 %copy-start.1 = (bf16[256,512]{1,0:T(8,128)(2,1)S(1)}, bf16[256,512]{1,0:T(8,128)(2,1)}, u32[]{:S(2)}) copy-start(bf16[256,512]{1,0:T(8,128)(2,1)} %value_hbm.1) | copy-start | bytes 786436
  45.7 10.4 %copy-start.9 = (s32[8]{0:T(128)S(1)}, s32[8]{0:T(128)}, u32[]{:S(2)}) copy-start(s32[8]{0:T(128)} %starts_hbm.1) | copy-start | bytes 100
  45.7 10.4 %copy-start.10 = (s32[8]{0:T(128)S(1)}, s32[8]{0:T(128)}, u32[]{:S(2)}) copy-start(s32[8]{0:T(128)} %domains_hbm.1) | copy-start | bytes 100
  45.7 16.3 %collective-permute-start.3 = (bf16[2,256,256]{2,1,0:T(8,128)(2,1)S(1)}, bf16[2,256,256]{2,1,0:T(8,128)(2,1)S(1)}, u32[]{:S(2)}, u32[]{:S(2)}) collective-permute-start(bf16[2,256,256]{2,1,0:T(8,128)(2,1)S(1)} %pad_maximum_fusion.refs_1_), channel_id=1, source_target_pairs={{0,3},{1,0},{2,1},{3,2},{4,7},{5,4},{6,5},{7,6},{8,11},{9,8},{10,9... | collective-permute-start | bytes 786440 | tf_op jit(solution)/shard_map/ppermute | solution.py:262
  50.5 12.6 %collective-permute-start.2 = (bf16[2,256,256]{2,1,0:T(8,128)(2,1)S(1)}, bf16[2,256,256]{2,1,0:T(8,128)(2,1)S(1)}, u32[]{:S(2)}, u32[]{:S(2)}) collective-permute-start(bf16[2,256,256]{2,1,0:T(8,128)(2,1)S(1)} %pad_maximum_fusion.refs_1_), channel_id=1, source_target_pairs={{0,2},{1,3},{2,0},{3,1},{4,6},{5,7},{6,4},{7,5},{8,10},{9,11},{10,... | collective-permute-start | bytes 786440 | tf_op jit(solution)/shard_map/ppermute | solution.py:262
  53.2 14.4 %collective-permute-start.1 = (bf16[2,256,256]{2,1,0:T(8,128)(2,1)S(1)}, bf16[2,256,256]{2,1,0:T(8,128)(2,1)S(1)}, u32[]{:S(2)}, u32[]{:S(2)}) collective-permute-start(bf16[2,256,256]{2,1,0:T(8,128)(2,1)S(1)} %pad_maximum_fusion.refs_1_), channel_id=1, source_target_pairs={{0,1},{1,2},{2,3},{3,0},{4,5},{5,6},{6,7},{7,4},{8,9},{9,10},{10,1... | collective-permute-start | bytes 786440 | tf_op jit(solution)/shard_map/ppermute | solution.py:262
  94.5 15.1 %copy-start.4 = (f32[512,16]{0,1:T(8,128)S(1)}, f32[512,16]{0,1:T(8,128)}, u32[]{:S(2)}) copy-start(f32[512,16]{0,1:T(8,128)} %param.19) | copy-start | bytes 98308
  94.5 15.1 %copy-start.5 = (f32[512,16]{0,1:T(8,128)S(1)}, f32[512,16]{0,1:T(8,128)}, u32[]{:S(2)}) copy-start(f32[512,16]{0,1:T(8,128)} %param.20) | copy-start | bytes 98308
  94.5 15.1 %copy-start.6 = (f32[512,16]{0,1:T(8,128)S(1)}, f32[512,16]{0,1:T(8,128)}, u32[]{:S(2)}) copy-start(f32[512,16]{0,1:T(8,128)} %param.21) | copy-start | bytes 98308

commit v5 on v4

--- a/solution.py
+++ b/solution.py
@@ -160,10 +160,11 @@
     shared_ref[row_count:, :] = jnp.broadcast_to(line, (16, width)).astype(bf16)
 
 
-def turn_kernel(cotangent_ref, core_ref, own_ref, other_ref, turned_ref, *, owned):
+def turn_kernel(cotangent_ref, own_ref, other_ref, turned_ref, *, owned):
     width = cotangent_ref.shape[1]
     turned_ref[...] = cotangent_ref[...].T
-    for core, out_ref in ((core_ref[0], own_ref), (1 - core_ref[0], other_ref)):
+    own = lax.axis_index("core")
+    for core, out_ref in ((own, own_ref), (1 - own, other_ref)):
         for pair in range(width // (2 * owned)):
             start = pl.multiple_of(2 * pair * owned + core * owned, owned)
             out_ref[pair * owned : (pair + 1) * owned] = turned_ref[pl.ds(start, owned), :]
@@ -231,15 +232,13 @@
     rows, heads = HEAD_DIM // blocks, width // HEAD_DIM
     V, S = VMEM_SPEC, SMEM_SPEC
 
-    core, group = lax.axis_index("core"), lax.axis_index("group")
-    place = jnp.stack([core, group]).astype(i32)
     own_half, other_half = pl.pallas_call(
         lambda *refs: turn_kernel(*refs, owned=owned),
         out_shape=(shape((width // 2, row_count), bf16),) * 2,
-        in_specs=[V, S], out_specs=(V, V),
+        in_specs=[V], out_specs=(V, V),
         scratch_shapes=[pltpu.VMEM((width, row_count), bf16)],
         compiler_params=SMALL, name="turn",
-    )(cotangent, place)
+    )(cotangent)
     states = pl.pallas_call(
         state_kernel,
         out_shape=pltpu.VMEM((HEAD_DIM, 1, width + LANES), f32),
@@ -260,14 +259,15 @@
     turned = [halves]
     for k in range(1, groups):
         turned.append(lax.ppermute(halves, "group", [(g, (g + k) % groups) for g in range(groups)]))
-    inner, first, lines = pl.pallas_call(
+    inner_call = pl.pallas_call(
         inner_kernel,
         out_shape=(
             shape((row_count, width), f32), shape((row_count, width), bf16), shape((8, width), f32)
         ),
         in_specs=[V, V, V, V, S, S, S], out_specs=(V, V, V),
         compiler_params=SMALL, name="inner",
-    )(
+    )
+    inner, first, lines = inner_call(
         queries, key_rows, value_rows, out_gain.reshape(1, width),
         doc_starts, doc_domains, domain_weights,
     )

time: 111 us -> 111 us (level)
  no operation moved by 1% of the time
where the time goes in v5:
time: 111 us; the launch traced here: 110 us
  blocking collectives  42.7 us (38%)
  starting transfers between devices  36.5 us (33%)
  waiting for transfers between devices  21.3 us (19%)
  Pallas kernels  8.77 us (8%)
    all_to_all x1, blocking collectives, on_device(): lax.all_to_all(partial.reshape(side, side * owned, width), ('chip', 'core...  25.4 us
    all_to_all x1, starting transfers between devices, on_device(): states = lax.all_to_all(states, ('chip', 'core'), 0, 0, tiled=True)  17.5 us
    all_to_all x1, blocking collectives, on_device(): lax.all_to_all(partial.reshape(side, owned, width), ('chip', 'core'), 0,...  15.1 us
    all_to_all x1, waiting for transfers between devices, on_device(): states = lax.all_to_all(states, ('chip', 'core'), 0, 0, tiled=True)  13.9 us
    ppermute x3, starting transfers between devices, on_device(): lax.ppermute(halves, 'group', [(g, (g + k) % groups) for g in range(group...  10.3 us
    ppermute x3, waiting for transfers between devices, on_device(): lax.ppermute(halves, 'group', [(g, (g + k) % groups) for g in range(group...  7.18 us
    all_to_all x1, starting transfers between devices, on_device(): carried = lax.all_to_all(carried, ('chip', 'core'), 0, 0, tiled=True)  6.68 us
    pallas_call x1, Pallas kernels, on_device(): carried, weight_in = carry_call(domain_weights.reshape(1, -1), states)  2.35 us
  transfers between devices with their start and end apart: 6, of which 5 were waited for; matrix products, arithmetic and copies ran while one was open for 0% of the time, Pallas kernels for 4%

profile of v5, /device:TPU:8, one launch (start us, length us, event | category | flops | bytes accessed | tf_op | source)
XLA Modules:
  0.0 110.3 jit_solution(1974311379789786466)
XLA Ops:
  0.6 2.3 %state.1 = f32[128,1,640]{2,1,0:T(1,128)} custom-call(bf16[256,512]{1,0:T(8,128)(2,1)} %key_hbm.1, bf16[256,512]{1,0:T(8,128)(2,1)} %value_hbm.1, s32[8]{0:T(128)} %starts_hbm.1, s32[8]{0:T(128)} %domains_hbm.1), custom_call_target="tpu_custom_call" | custom-call | tf_op jit(solution)/shard_map/state/pallas_call | solution.py:242
  2.9 0.0 copy-start.2
  2.9 17.5 %all-to-all-start = ((f32[128,1,640]{2,1,0:T(1,128)}), f32[128,1,640]{2,1,0:T(1,128)S(1)}, u32[]{:S(2)}, u32[]{:S(2)}) async-start(f32[128,1,640]{2,1,0:T(1,128)} %state.1), calls=%async_computation | async-start | bytes 655360 | tf_op jit(solution)/shard_map/all_to_all | solution.py:256
  20.4 0.0 copy-done.2
  20.4 0.1 turn.1
  20.6 0.0 copy-start.8
  20.6 2.0 %collective-permute-start = (bf16[256,256]{1,0:T(8,128)(2,1)S(1)}, bf16[256,256]{1,0:T(8,128)(2,1)S(1)}, u32[]{:S(2)}, u32[]{:S(2)}) collective-permute-start(bf16[256,256]{1,0:T(8,128)(2,1)S(1)} %get-tuple-element.22), channel_id=1, source_target_pairs={{0,4},{4,0},{1,5},{5,1},{2,6},{6,2},{3,7},{7,3},{8,12},{12,8},{9,1... | collective-permute-start | bytes 393224 | tf_op jit(solution)/shard_map/ppermute | solution.py:257
  22.6 13.9 %all-to-all-done.states_ref = f32[128,1,640]{2,1,0:T(1,128)S(1)} async-done(((f32[128,1,640]{2,1,0:T(1,128)}), f32[128,1,640]{2,1,0:T(1,128)S(1)}, u32[]{:S(2)}, u32[]{:S(2)}) %all-to-all-start) | async-done | bytes 327712 | tf_op jit(solution)/shard_map/all_to_all | solution.py:256
  36.5 0.0 copy-done.8
  36.5 2.3 %carry.1 = (bf16[128,4,128]{2,1,0:T(4,128)(2,1)}, f32[8,128]{1,0:T(8,128)S(1)}) custom-call(s32[1,8]{1,0:T(1,128)S(1)} %bitcast.21, f32[128,1,640]{2,1,0:T(1,128)S(1)} %all-to-all-done.states_ref), custom_call_target="tpu_custom_call" | custom-call | tf_op jit(solution)/shard_map/carry/pallas_call | solution.py:283
  38.9 0.0 copy-start.3
  38.9 6.7 %all-to-all-start.1 = ((bf16[128,4,128]{2,1,0:T(4,128)(2,1)}), bf16[128,4,128]{2,1,0:T(4,128)(2,1)S(1)}, u32[]{:S(2)}, u32[]{:S(2)}) async-start(bf16[128,4,128]{2,1,0:T(4,128)(2,1)} %get-tuple-element.18), calls=%async_computation.1 | async-start | bytes 262144 | tf_op jit(solution)/shard_map/all_to_all | solution.py:284
  45.6 0.0 collective-permute-done
  45.6 0.0 copy-start.7
  45.6 0.0 copy-start
  45.6 0.0 copy-start.1
  45.7 0.0 copy-start.9
  45.7 0.0 copy-start.10
  45.7 4.8 %collective-permute-start.3 = (bf16[2,256,256]{2,1,0:T(8,128)(2,1)S(1)}, bf16[2,256,256]{2,1,0:T(8,128)(2,1)S(1)}, u32[]{:S(2)}, u32[]{:S(2)}) collective-permute-start(bf16[2,256,256]{2,1,0:T(8,128)(2,1)S(1)} %pad_maximum_fusion.refs_1_), channel_id=1, source_target_pairs={{0,3},{1,0},{2,1},{3,2},{4,7},{5,4},{6,5},{7,6},{8,11},{9,8},{10,9... | collective-permute-start | bytes 786440 | tf_op jit(solution)/shard_map/ppermute | solution.py:261
  50.5 2.7 %collective-permute-start.2 = (bf16[2,256,256]{2,1,0:T(8,128)(2,1)S(1)}, bf16[2,256,256]{2,1,0:T(8,128)(2,1)S(1)}, u32[]{:S(2)}, u32[]{:S(2)}) collective-permute-start(bf16[2,256,256]{2,1,0:T(8,128)(2,1)S(1)} %pad_maximum_fusion.refs_1_), channel_id=1, source_target_pairs={{0,2},{1,3},{2,0},{3,1},{4,6},{5,7},{6,4},{7,5},{8,10},{9,11},{10,... | collective-permute-start | bytes 786440 | tf_op jit(solution)/shard_map/ppermute | solution.py:261
  53.2 2.8 %collective-permute-start.1 = (bf16[2,256,256]{2,1,0:T(8,128)(2,1)S(1)}, bf16[2,256,256]{2,1,0:T(8,128)(2,1)S(1)}, u32[]{:S(2)}, u32[]{:S(2)}) collective-permute-start(bf16[2,256,256]{2,1,0:T(8,128)(2,1)S(1)} %pad_maximum_fusion.refs_1_), channel_id=1, source_target_pairs={{0,1},{1,2},{2,3},{3,0},{4,5},{5,6},{6,7},{7,4},{8,9},{9,10},{10,1... | collective-permute-start | bytes 786440 | tf_op jit(solution)/shard_map/ppermute | solution.py:261
  56.0 0.0 copy-done.3
  56.0 0.0 copy-done.7
  56.0 0.0 copy-done
  56.0 0.0 copy-done.1
  56.1 0.0 copy-done.9
  56.1 0.0 copy-done.10
  56.1 1.2 %inner.1 = (f32[256,512]{1,0:T(8,128)S(1)}, bf16[256,512]{1,0:T(8,128)(2,1)S(1)}, f32[8,512]{1,0:T(8,128)S(1)}) custom-call(bf16[256,512]{1,0:T(8,128)(2,1)S(1)} %copy-done.3, bf16[256,512]{1,0:T(8,128)(2,1)S(1)} %copy-done, bf16[256,512]{1,0:T(8,128)(2,1)S(1)} %copy-done.1, f32[1,512]{1,0:T(1,128)S(1)} %bitcast.20, s32[8]{0:T(128)S(1)} %copy-done.9, ...), custom_call_target="tpu_custom_call" | custom-call | tf_op jit(solution)/shard_map/inner/pallas_call | solution.py:270
  57.3 0.3 all-to-all-done.1.carried_ref
  57.6 0.6 attention.1
  58.2 2.2 %all-gather = bf16[544,512]{1,0:T(8,128)(2,1)S(1)} all-gather(bf16[272,512]{1,0:T(8,128)(2,1)S(1)} %attention.1), channel_id=2, replica_groups=mesh['chip'=64,'core'=2,'group'=4] {'core'}, dimensions={0}, use_global_device_ids=true | all-gather | bytes 835584 | tf_op jit(solution)/shard_map/all_gather | solution.py:292
  60.4 1.6 %collective-permute-done.3.refs_4_ = bf16[2,256,256]{2,1,0:T(8,128)(2,1)S(1)} collective-permute-done((bf16[2,256,256]{2,1,0:T(8,128)(2,1)S(1)}, bf16[2,256,256]{2,1,0:T(8,128)(2,1)S(1)}, u32[]{:S(2)}, u32[]{:S(2)}) %collective-permute-start.3) | collective-permute-done | bytes 262176 | tf_op jit(solution)/shard_map/ppermute | solution.py:261
  62.0 1.1 %collective-permute-done.2.refs_3_ = bf16[2,256,256]{2,1,0:T(8,128)(2,1)S(1)} collective-permute-done((bf16[2,256,256]{2,1,0:T(8,128)(2,1)S(1)}, bf16[2,256,256]{2,1,0:T(8,128)(2,1)S(1)}, u32[]{:S(2)}, u32[]{:S(2)}) %collective-permute-start.2) | collective-permute-done | bytes 262176 | tf_op jit(solution)/shard_map/ppermute | solution.py:261
  63.1 4.4 %collective-permute-done.1.refs_2_ = bf16[2,256,256]{2,1,0:T(8,128)(2,1)S(1)} collective-permute-done((bf16[2,256,256]{2,1,0:T(8,128)(2,1)S(1)}, bf16[2,256,256]{2,1,0:T(8,128)(2,1)S(1)}, u32[]{:S(2)}, u32[]{:S(2)}) %collective-permute-start.1) | collective-permute-done | bytes 262176 | tf_op jit(solution)/shard_map/ppermute | solution.py:261
  67.6 1.4 %gradient.1 = (bf16[1024,512]{1,0:T(8,128)(2,1)S(1)}, bf16[256,512]{1,0:T(8,128)(2,1)}) custom-call(bf16[2,272,512]{2,1,0:T(8,128)(2,1)S(1)} %bitcast.13, bf16[2,256,256]{2,1,0:T(8,128)(2,1)S(1)} %pad_maximum_fusion.refs_1_, bf16[2,256,256]{2,1,0:T(8,128)(2,1)S(1)} %collective-permute-done.1.refs_2_, ...), custom_call_target="tpu_custom_call" | custom-call | tf_op jit(solution)/shard_map/gradient/pallas_call | solution.py:294
  69.0 25.4 %all_to_all.20.parts_ref = bf16[8,128,512]{2,1,0:T(8,128)(2,1)S(1)} all-to-all(bf16[8,128,512]{2,1,0:T(8,128)(2,1)S(1)} %bitcast.14), channel_id=1, replica_groups={{0,8,16,24,32,40,48,56},{64,72,80,88,96,104,112,120},{128,136,144,152,1..., dimensions={0} | all-to-all | bytes 2097152 | tf_op jit(solution)/shard_map/all_to_all | solution.py:307
  94.4 0.1 sum.1
  94.5 0.0 copy-start.4
  94.5 0.0 copy-start.5
  94.5 0.0 copy-start.6
  94.5 15.1 %all_to_all.21.parts_ref = bf16[8,16,512]{2,1,0:T(8,128)(2,1)S(1)} all-to-all(bf16[8,16,512]{2,1,0:T(8,128)(2,1)S(1)} %bitcast.15), channel_id=1, replica_groups={{0,64,128,192,256,320,384,448},{8,72,136,200,264,328,392,456},{16,80,14..., dimensions={0} | all-to-all | bytes 262144 | tf_op jit(solution)/shard_map/all_to_all | solution.py:316
  109.6 0.0 copy-done.4
  109.6 0.0 copy-done.5
  109.6 0.0 copy-done.6
  109.6 0.7 update.1
  (1 shorter events, 0.0 us)
Async XLA Ops:
  2.9 17.5 %copy-start.2 = (bf16[256,512]{1,0:T(8,128)(2,1)S(1)}, bf16[256,512]{1,0:T(8,128)(2,1)}, u32[]{:S(2)}) copy-start(bf16[256,512]{1,0:T(8,128)(2,1)} %refs_0_.1) | copy-start | bytes 786436
  2.9 33.6 %all-to-all-start = ((f32[128,1,640]{2,1,0:T(1,128)}), f32[128,1,640]{2,1,0:T(1,128)S(1)}, u32[]{:S(2)}, u32[]{:S(2)}) async-start(f32[128,1,640]{2,1,0:T(1,128)} %state.1), calls=%async_computation | async-start | bytes 655360 | tf_op jit(solution)/shard_map/all_to_all | solution.py:256
  20.6 16.0 %copy-start.8 = (s32[8]{0:T(128)S(1)}, s32[8]{0:T(128)}, u32[]{:S(2)}) copy-start(s32[8]{0:T(128)} %weights_ref.1) | copy-start | bytes 100
  20.6 25.0 %collective-permute-start = (bf16[256,256]{1,0:T(8,128)(2,1)S(1)}, bf16[256,256]{1,0:T(8,128)(2,1)S(1)}, u32[]{:S(2)}, u32[]{:S(2)}) collective-permute-start(bf16[256,256]{1,0:T(8,128)(2,1)S(1)} %get-tuple-element.22), channel_id=1, source_target_pairs={{0,4},{4,0},{1,5},{5,1},{2,6},{6,2},{3,7},{7,3},{8,12},{12,8},{9,1... | collective-permute-start | bytes 393224 | tf_op jit(solution)/shard_map/ppermute | solution.py:257
  38.9 17.1 %copy-start.3 = (bf16[256,512]{1,0:T(8,128)(2,1)S(1)}, bf16[256,512]{1,0:T(8,128)(2,1)}, u32[]{:S(2)}) copy-start(bf16[256,512]{1,0:T(8,128)(2,1)} %query_ref.1) | copy-start | bytes 786436
  38.9 18.7 %all-to-all-start.1 = ((bf16[128,4,128]{2,1,0:T(4,128)(2,1)}), bf16[128,4,128]{2,1,0:T(4,128)(2,1)S(1)}, u32[]{:S(2)}, u32[]{:S(2)}) async-start(bf16[128,4,128]{2,1,0:T(4,128)(2,1)} %get-tuple-element.18), calls=%async_computation.1 | async-start | bytes 262144 | tf_op jit(solution)/shard_map/all_to_all | solution.py:284
  45.6 10.4 %copy-start.7 = (f32[512]{0:T(512)S(1)}, f32[512]{0:T(512)}, u32[]{:S(2)}) copy-start(f32[512]{0:T(512)} %param.14) | copy-start | bytes 6148
  45.6 10.4 %copy-start = (bf16[256,512]{1,0:T(8,128)(2,1)S(1)}, bf16[256,512]{1,0:T(8,128)(2,1)}, u32[]{:S(2)}) copy-start(bf16[256,512]{1,0:T(8,128)(2,1)} %key_hbm.1) | copy-start | bytes 786436
  45.6 10.4 %copy-start.1 = (bf16[256,512]{1,0:T(8,128)(2,1)S(1)}, bf16[256,512]{1,0:T(8,128)(2,1)}, u32[]{:S(2)}) copy-start(bf16[256,512]{1,0:T(8,128)(2,1)} %value_hbm.1) | copy-start | bytes 786436
  45.7 10.4 %copy-start.9 = (s32[8]{0:T(128)S(1)}, s32[8]{0:T(128)}, u32[]{:S(2)}) copy-start(s32[8]{0:T(128)} %starts_hbm.1) | copy-start | bytes 100
  45.7 10.4 %copy-start.10 = (s32[8]{0:T(128)S(1)}, s32[8]{0:T(128)}, u32[]{:S(2)}) copy-start(s32[8]{0:T(128)} %domains_hbm.1) | copy-start | bytes 100
  45.7 16.3 %collective-permute-start.3 = (bf16[2,256,256]{2,1,0:T(8,128)(2,1)S(1)}, bf16[2,256,256]{2,1,0:T(8,128)(2,1)S(1)}, u32[]{:S(2)}, u32[]{:S(2)}) collective-permute-start(bf16[2,256,256]{2,1,0:T(8,128)(2,1)S(1)} %pad_maximum_fusion.refs_1_), channel_id=1, source_target_pairs={{0,3},{1,0},{2,1},{3,2},{4,7},{5,4},{6,5},{7,6},{8,11},{9,8},{10,9... | collective-permute-start | bytes 786440 | tf_op jit(solution)/shard_map/ppermute | solution.py:261
  50.5 12.6 %collective-permute-start.2 = (bf16[2,256,256]{2,1,0:T(8,128)(2,1)S(1)}, bf16[2,256,256]{2,1,0:T(8,128)(2,1)S(1)}, u32[]{:S(2)}, u32[]{:S(2)}) collective-permute-start(bf16[2,256,256]{2,1,0:T(8,128)(2,1)S(1)} %pad_maximum_fusion.refs_1_), channel_id=1, source_target_pairs={{0,2},{1,3},{2,0},{3,1},{4,6},{5,7},{6,4},{7,5},{8,10},{9,11},{10,... | collective-permute-start | bytes 786440 | tf_op jit(solution)/shard_map/ppermute | solution.py:261
  53.2 14.4 %collective-permute-start.1 = (bf16[2,256,256]{2,1,0:T(8,128)(2,1)S(1)}, bf16[2,256,256]{2,1,0:T(8,128)(2,1)S(1)}, u32[]{:S(2)}, u32[]{:S(2)}) collective-permute-start(bf16[2,256,256]{2,1,0:T(8,128)(2,1)S(1)} %pad_maximum_fusion.refs_1_), channel_id=1, source_target_pairs={{0,1},{1,2},{2,3},{3,0},{4,5},{5,6},{6,7},{7,4},{8,9},{9,10},{10,1... | collective-permute-start | bytes 786440 | tf_op jit(solution)/shard_map/ppermute | solution.py:261
  94.5 15.1 %copy-start.4 = (f32[512,16]{0,1:T(8,128)S(1)}, f32[512,16]{0,1:T(8,128)}, u32[]{:S(2)}) copy-start(f32[512,16]{0,1:T(8,128)} %param.19) | copy-start | bytes 98308
  94.5 15.1 %copy-start.5 = (f32[512,16]{0,1:T(8,128)S(1)}, f32[512,16]{0,1:T(8,128)}, u32[]{:S(2)}) copy-start(f32[512,16]{0,1:T(8,128)} %param.20) | copy-start | bytes 98308
  94.5 15.1 %copy-start.6 = (f32[512,16]{0,1:T(8,128)S(1)}, f32[512,16]{0,1:T(8,128)}, u32[]{:S(2)}) copy-start(f32[512,16]{0,1:T(8,128)} %param.21) | copy-start | bytes 98308

commit v6 on v5

--- a/solution.py
+++ b/solution.py
@@ -33,24 +33,13 @@
     return total
 
 
-def started_and_domain(starts_ref, domains_ref, row_count):
-    slots = starts_ref.shape[0]
-    started = jnp.int32(0)
-    for slot in range(slots):
-        started = started + (starts_ref[slot] < row_count).astype(i32)
-    last_domain = jnp.int32(0)
-    for slot in range(slots):
-        last_domain = last_domain + jnp.where(slot == started - 1, domains_ref[slot], 0)
-    return started, last_domain
-
-
 def dot(a, b, contract):
     return lax.dot_general(a, b, (contract, ((), ())), preferred_element_type=f32)
 
 
 def state_kernel(
-    key_hbm, value_hbm, starts_hbm, domains_hbm, out_ref,
-    key_ref, value_ref, starts_ref, domains_ref, arrived,
+    key_hbm, value_hbm, starts_hbm, domains_hbm, out_hbm,
+    key_ref, value_ref, starts_ref, domains_ref, out_ref, arrived, left,
 ):
     copies = [
         pltpu.make_async_copy(source, target, arrived.at[which])
@@ -61,20 +50,41 @@
     ]
     for copy in copies:
         copy.start()
-    for copy in copies:
-        copy.wait()
     row_count, width = key_ref.shape
-    started, last_domain = started_and_domain(starts_ref, domains_ref, row_count)
-    in_tail = docs_along(starts_ref, (row_count, HEAD_DIM), 0) == started
-    for head in range(width // HEAD_DIM):
-        cols = slice(head * HEAD_DIM, (head + 1) * HEAD_DIM)
-        keys = jnp.where(in_tail, key_ref[:, cols].astype(f32), 0.0).astype(bf16)
-        out_ref[:, 0, cols] = dot(keys, value_ref[:, cols], ((0,), (0,)))
+    heads = width // HEAD_DIM
+    saves = [
+        pltpu.make_async_copy(out_ref.at[:, :, cols], out_hbm.at[:, :, cols], left.at[which])
+        for which, cols in enumerate(
+            pl.ds(head * HEAD_DIM, HEAD_DIM) for head in range(heads + 1)
+        )
+    ]
+    copies[0].wait()
+    copies[1].wait()
+    starts = starts_ref[...]
+    slots = starts.shape[1]
+    started = jnp.sum((starts < row_count).astype(i32), axis=1, keepdims=True)
+    last = iota((1, slots), 1) == started - 1
+    last_domain = jnp.sum(jnp.where(last, domains_ref[...], 0), axis=1, keepdims=True)
     lane = iota((HEAD_DIM, LANES), 1)
     flag = (started > 0).astype(f32)
     out_ref[:, 0, width:] = jnp.where(
         lane == 0, flag, jnp.where(lane == 1, last_domain.astype(f32), 0.0)
     )
+    saves[heads].start()
+    positions = iota((row_count, HEAD_DIM), 0)
+    docs = jnp.zeros((row_count, HEAD_DIM), i32)
+    for slot in range(slots):
+        docs = docs + (starts[:, slot : slot + 1] <= positions).astype(i32)
+    in_tail = docs == started
+    copies[2].wait()
+    copies[3].wait()
+    for head in range(heads):
+        cols = slice(head * HEAD_DIM, (head + 1) * HEAD_DIM)
+        keys = jnp.where(in_tail, key_ref[:, cols].astype(f32), 0.0).astype(bf16)
+        out_ref[:, 0, cols] = dot(keys, value_ref[:, cols], ((0,), (0,)))
+        saves[head].start()
+    for save in saves:
+        save.wait()
 
 
 def carry_kernel(weights_ref, states_ref, carried_ref, weight_ref, total_ref):
@@ -241,17 +251,20 @@
     )(cotangent)
     states = pl.pallas_call(
         state_kernel,
-        out_shape=pltpu.VMEM((HEAD_DIM, 1, width + LANES), f32),
-        in_specs=[HBM_SPEC] * 4, out_specs=V,
+        out_shape=shape((HEAD_DIM, 1, width + LANES), f32),
+        in_specs=[HBM_SPEC] * 4, out_specs=HBM_SPEC,
         scratch_shapes=[
             pltpu.VMEM(key_rows.shape, bf16), pltpu.VMEM(value_rows.shape, bf16),
-            pltpu.SMEM(doc_starts.shape, i32), pltpu.SMEM(doc_domains.shape, i32),
-            pltpu.SemaphoreType.DMA((4,)),
+            pltpu.VMEM((1, doc_starts.shape[0]), i32), pltpu.VMEM((1, doc_starts.shape[0]), i32),
+            pltpu.VMEM((HEAD_DIM, 1, width + LANES), f32),
+            pltpu.SemaphoreType.DMA((4,)), pltpu.SemaphoreType.DMA((heads + 1,)),
         ],
         compiler_params=SMALL, name="state",
     )(*(
         pltpu.with_memory_space_constraint(operand, pltpu.HBM)
-        for operand in (key_rows, value_rows, doc_starts, doc_domains)
+        for operand in (
+            key_rows, value_rows, doc_starts.reshape(1, -1), doc_domains.reshape(1, -1)
+        )
     ))
     states = lax.all_to_all(states, ("chip", "core"), 0, 0, tiled=True)
     partner_half = lax.ppermute(other_half, "core", [(0, 1), (1, 0)])

time: 111 us -> 111 us (level)
  no operation moved by 1% of the time
where the time goes in v6:
time: 111 us; the launch traced here: 110 us
  blocking collectives  42.7 us (38%)
  starting transfers between devices  36.5 us (33%)
  waiting for transfers between devices  21.3 us (19%)
  Pallas kernels  8.66 us (8%)
    all_to_all x1, blocking collectives, on_device(): lax.all_to_all(partial.reshape(side, side * owned, width), ('chip', 'core...  25.4 us
    all_to_all x1, starting transfers between devices, on_device(): states = lax.all_to_all(states, ('chip', 'core'), 0, 0, tiled=True)  17.5 us
    all_to_all x1, blocking collectives, on_device(): lax.all_to_all(partial.reshape(side, owned, width), ('chip', 'core'), 0,...  15.1 us
    all_to_all x1, waiting for transfers between devices, on_device(): states = lax.all_to_all(states, ('chip', 'core'), 0, 0, tiled=True)  13.9 us
    ppermute x3, starting transfers between devices, on_device(): lax.ppermute(halves, 'group', [(g, (g + k) % groups) for g in range(group...  10.3 us
    ppermute x3, waiting for transfers between devices, on_device(): lax.ppermute(halves, 'group', [(g, (g + k) % groups) for g in range(group...  7.18 us
    all_to_all x1, starting transfers between devices, on_device(): carried = lax.all_to_all(carried, ('chip', 'core'), 0, 0, tiled=True)  6.68 us
    pallas_call x1, Pallas kernels, on_device(): carried, weight_in = carry_call(domain_weights.reshape(1, -1), states)  2.35 us
  transfers between devices with their start and end apart: 6, of which 5 were waited for; matrix products, arithmetic and copies ran while one was open for 0% of the time, Pallas kernels for 4%

profile of v6, /device:TPU:8, one launch (start us, length us, event | category | flops | bytes accessed | tf_op | source)
XLA Modules:
  0.0 110.2 jit_solution(8833581601941892)
XLA Ops:
  0.6 2.1 %state.1 = f32[128,1,640]{2,1,0:T(1,128)} custom-call(bf16[256,512]{1,0:T(8,128)(2,1)} %key_hbm.1, bf16[256,512]{1,0:T(8,128)(2,1)} %value_hbm.1, s32[1,8]{1,0:T(1,128)} %bitcast.24, s32[1,8]{1,0:T(1,128)} %bitcast.25), custom_call_target="tpu_custom_call" | custom-call | tf_op jit(solution)/shard_map/state/pallas_call | solution.py:252
  2.8 0.0 copy-start.2
  2.8 17.5 %all-to-all-start = ((f32[128,1,640]{2,1,0:T(1,128)}), f32[128,1,640]{2,1,0:T(1,128)S(1)}, u32[]{:S(2)}, u32[]{:S(2)}) async-start(f32[128,1,640]{2,1,0:T(1,128)} %state.1), calls=%async_computation | async-start | bytes 655360 | tf_op jit(solution)/shard_map/all_to_all | solution.py:269
  20.3 0.0 copy-done.2
  20.3 0.1 turn.1
  20.5 0.0 copy-start.8
  20.5 2.0 %collective-permute-start = (bf16[256,256]{1,0:T(8,128)(2,1)S(1)}, bf16[256,256]{1,0:T(8,128)(2,1)S(1)}, u32[]{:S(2)}, u32[]{:S(2)}) collective-permute-start(bf16[256,256]{1,0:T(8,128)(2,1)S(1)} %get-tuple-element.22), channel_id=1, source_target_pairs={{0,4},{4,0},{1,5},{5,1},{2,6},{6,2},{3,7},{7,3},{8,12},{12,8},{9,1... | collective-permute-start | bytes 393224 | tf_op jit(solution)/shard_map/ppermute | solution.py:270
  22.5 13.9 %all-to-all-done.states_ref = f32[128,1,640]{2,1,0:T(1,128)S(1)} async-done(((f32[128,1,640]{2,1,0:T(1,128)}), f32[128,1,640]{2,1,0:T(1,128)S(1)}, u32[]{:S(2)}, u32[]{:S(2)}) %all-to-all-start) | async-done | bytes 327712 | tf_op jit(solution)/shard_map/all_to_all | solution.py:269
  36.4 0.0 copy-done.8
  36.4 2.3 %carry.1 = (bf16[128,4,128]{2,1,0:T(4,128)(2,1)}, f32[8,128]{1,0:T(8,128)S(1)}) custom-call(s32[1,8]{1,0:T(1,128)S(1)} %bitcast.23, f32[128,1,640]{2,1,0:T(1,128)S(1)} %all-to-all-done.states_ref), custom_call_target="tpu_custom_call" | custom-call | tf_op jit(solution)/shard_map/carry/pallas_call | solution.py:296
  38.8 0.0 copy-start.3
  38.8 6.7 %all-to-all-start.1 = ((bf16[128,4,128]{2,1,0:T(4,128)(2,1)}), bf16[128,4,128]{2,1,0:T(4,128)(2,1)S(1)}, u32[]{:S(2)}, u32[]{:S(2)}) async-start(bf16[128,4,128]{2,1,0:T(4,128)(2,1)} %get-tuple-element.18), calls=%async_computation.1 | async-start | bytes 262144 | tf_op jit(solution)/shard_map/all_to_all | solution.py:297
  45.5 0.0 collective-permute-done
  45.5 0.0 copy-start.7
  45.5 0.0 copy-start
  45.5 0.0 copy-start.1
  45.6 0.0 copy-start.9
  45.6 0.0 copy-start.10
  45.6 4.8 %collective-permute-start.3 = (bf16[2,256,256]{2,1,0:T(8,128)(2,1)S(1)}, bf16[2,256,256]{2,1,0:T(8,128)(2,1)S(1)}, u32[]{:S(2)}, u32[]{:S(2)}) collective-permute-start(bf16[2,256,256]{2,1,0:T(8,128)(2,1)S(1)} %pad_maximum_fusion.refs_1_), channel_id=1, source_target_pairs={{0,3},{1,0},{2,1},{3,2},{4,7},{5,4},{6,5},{7,6},{8,11},{9,8},{10,9... | collective-permute-start | bytes 786440 | tf_op jit(solution)/shard_map/ppermute | solution.py:274
  50.4 2.7 %collective-permute-start.2 = (bf16[2,256,256]{2,1,0:T(8,128)(2,1)S(1)}, bf16[2,256,256]{2,1,0:T(8,128)(2,1)S(1)}, u32[]{:S(2)}, u32[]{:S(2)}) collective-permute-start(bf16[2,256,256]{2,1,0:T(8,128)(2,1)S(1)} %pad_maximum_fusion.refs_1_), channel_id=1, source_target_pairs={{0,2},{1,3},{2,0},{3,1},{4,6},{5,7},{6,4},{7,5},{8,10},{9,11},{10,... | collective-permute-start | bytes 786440 | tf_op jit(solution)/shard_map/ppermute | solution.py:274
  53.1 2.8 %collective-permute-start.1 = (bf16[2,256,256]{2,1,0:T(8,128)(2,1)S(1)}, bf16[2,256,256]{2,1,0:T(8,128)(2,1)S(1)}, u32[]{:S(2)}, u32[]{:S(2)}) collective-permute-start(bf16[2,256,256]{2,1,0:T(8,128)(2,1)S(1)} %pad_maximum_fusion.refs_1_), channel_id=1, source_target_pairs={{0,1},{1,2},{2,3},{3,0},{4,5},{5,6},{6,7},{7,4},{8,9},{9,10},{10,1... | collective-permute-start | bytes 786440 | tf_op jit(solution)/shard_map/ppermute | solution.py:274
  55.9 0.0 copy-done.3
  55.9 0.0 copy-done.7
  55.9 0.0 copy-done
  55.9 0.0 copy-done.1
  55.9 0.0 copy-done.9
  56.0 0.0 copy-done.10
  56.0 1.2 %inner.1 = (f32[256,512]{1,0:T(8,128)S(1)}, bf16[256,512]{1,0:T(8,128)(2,1)S(1)}, f32[8,512]{1,0:T(8,128)S(1)}) custom-call(bf16[256,512]{1,0:T(8,128)(2,1)S(1)} %copy-done.3, bf16[256,512]{1,0:T(8,128)(2,1)S(1)} %copy-done, bf16[256,512]{1,0:T(8,128)(2,1)S(1)} %copy-done.1, f32[1,512]{1,0:T(1,128)S(1)} %bitcast.22, s32[8]{0:T(128)S(1)} %copy-done.9, ...), custom_call_target="tpu_custom_call" | custom-call | tf_op jit(solution)/shard_map/inner/pallas_call | solution.py:283
  57.2 0.3 all-to-all-done.1.carried_ref
  57.4 0.6 attention.1
  58.1 2.2 %all-gather = bf16[544,512]{1,0:T(8,128)(2,1)S(1)} all-gather(bf16[272,512]{1,0:T(8,128)(2,1)S(1)} %attention.1), channel_id=2, replica_groups=mesh['chip'=64,'core'=2,'group'=4] {'core'}, dimensions={0}, use_global_device_ids=true | all-gather | bytes 835584 | tf_op jit(solution)/shard_map/all_gather | solution.py:305
  60.3 1.6 %collective-permute-done.3.refs_4_ = bf16[2,256,256]{2,1,0:T(8,128)(2,1)S(1)} collective-permute-done((bf16[2,256,256]{2,1,0:T(8,128)(2,1)S(1)}, bf16[2,256,256]{2,1,0:T(8,128)(2,1)S(1)}, u32[]{:S(2)}, u32[]{:S(2)}) %collective-permute-start.3) | collective-permute-done | bytes 262176 | tf_op jit(solution)/shard_map/ppermute | solution.py:274
  61.9 1.1 %collective-permute-done.2.refs_3_ = bf16[2,256,256]{2,1,0:T(8,128)(2,1)S(1)} collective-permute-done((bf16[2,256,256]{2,1,0:T(8,128)(2,1)S(1)}, bf16[2,256,256]{2,1,0:T(8,128)(2,1)S(1)}, u32[]{:S(2)}, u32[]{:S(2)}) %collective-permute-start.2) | collective-permute-done | bytes 262176 | tf_op jit(solution)/shard_map/ppermute | solution.py:274
  63.0 4.4 %collective-permute-done.1.refs_2_ = bf16[2,256,256]{2,1,0:T(8,128)(2,1)S(1)} collective-permute-done((bf16[2,256,256]{2,1,0:T(8,128)(2,1)S(1)}, bf16[2,256,256]{2,1,0:T(8,128)(2,1)S(1)}, u32[]{:S(2)}, u32[]{:S(2)}) %collective-permute-start.1) | collective-permute-done | bytes 262176 | tf_op jit(solution)/shard_map/ppermute | solution.py:274
  67.5 1.4 %gradient.1 = (bf16[1024,512]{1,0:T(8,128)(2,1)S(1)}, bf16[256,512]{1,0:T(8,128)(2,1)}) custom-call(bf16[2,272,512]{2,1,0:T(8,128)(2,1)S(1)} %bitcast.15, bf16[2,256,256]{2,1,0:T(8,128)(2,1)S(1)} %pad_maximum_fusion.refs_1_, bf16[2,256,256]{2,1,0:T(8,128)(2,1)S(1)} %collective-permute-done.1.refs_2_, ...), custom_call_target="tpu_custom_call" | custom-call | tf_op jit(solution)/shard_map/gradient/pallas_call | solution.py:307
  68.8 25.4 %all_to_all.20.parts_ref = bf16[8,128,512]{2,1,0:T(8,128)(2,1)S(1)} all-to-all(bf16[8,128,512]{2,1,0:T(8,128)(2,1)S(1)} %bitcast.16), channel_id=1, replica_groups={{0,8,16,24,32,40,48,56},{64,72,80,88,96,104,112,120},{128,136,144,152,1..., dimensions={0} | all-to-all | bytes 2097152 | tf_op jit(solution)/shard_map/all_to_all | solution.py:320
  94.2 0.1 sum.1
  94.4 0.0 copy-start.4
  94.4 0.0 copy-start.5
  94.4 0.0 copy-start.6
  94.4 15.1 %all_to_all.21.parts_ref = bf16[8,16,512]{2,1,0:T(8,128)(2,1)S(1)} all-to-all(bf16[8,16,512]{2,1,0:T(8,128)(2,1)S(1)} %bitcast.17), channel_id=1, replica_groups={{0,64,128,192,256,320,384,448},{8,72,136,200,264,328,392,456},{16,80,14..., dimensions={0} | all-to-all | bytes 262144 | tf_op jit(solution)/shard_map/all_to_all | solution.py:329
  109.5 0.0 copy-done.4
  109.5 0.0 copy-done.5
  109.5 0.0 copy-done.6
  109.5 0.7 update.1
  (1 shorter events, 0.0 us)
Async XLA Ops:
  2.8 17.5 %copy-start.2 = (bf16[256,512]{1,0:T(8,128)(2,1)S(1)}, bf16[256,512]{1,0:T(8,128)(2,1)}, u32[]{:S(2)}) copy-start(bf16[256,512]{1,0:T(8,128)(2,1)} %refs_0_.1) | copy-start | bytes 786436
  2.8 33.6 %all-to-all-start = ((f32[128,1,640]{2,1,0:T(1,128)}), f32[128,1,640]{2,1,0:T(1,128)S(1)}, u32[]{:S(2)}, u32[]{:S(2)}) async-start(f32[128,1,640]{2,1,0:T(1,128)} %state.1), calls=%async_computation | async-start | bytes 655360 | tf_op jit(solution)/shard_map/all_to_all | solution.py:269
  20.5 16.0 %copy-start.8 = (s32[8]{0:T(128)S(1)}, s32[8]{0:T(128)}, u32[]{:S(2)}) copy-start(s32[8]{0:T(128)} %weights_ref.1) | copy-start | bytes 100
  20.5 25.0 %collective-permute-start = (bf16[256,256]{1,0:T(8,128)(2,1)S(1)}, bf16[256,256]{1,0:T(8,128)(2,1)S(1)}, u32[]{:S(2)}, u32[]{:S(2)}) collective-permute-start(bf16[256,256]{1,0:T(8,128)(2,1)S(1)} %get-tuple-element.22), channel_id=1, source_target_pairs={{0,4},{4,0},{1,5},{5,1},{2,6},{6,2},{3,7},{7,3},{8,12},{12,8},{9,1... | collective-permute-start | bytes 393224 | tf_op jit(solution)/shard_map/ppermute | solution.py:270
  38.8 17.1 %copy-start.3 = (bf16[256,512]{1,0:T(8,128)(2,1)S(1)}, bf16[256,512]{1,0:T(8,128)(2,1)}, u32[]{:S(2)}) copy-start(bf16[256,512]{1,0:T(8,128)(2,1)} %query_ref.1) | copy-start | bytes 786436
  38.8 18.7 %all-to-all-start.1 = ((bf16[128,4,128]{2,1,0:T(4,128)(2,1)}), bf16[128,4,128]{2,1,0:T(4,128)(2,1)S(1)}, u32[]{:S(2)}, u32[]{:S(2)}) async-start(bf16[128,4,128]{2,1,0:T(4,128)(2,1)} %get-tuple-element.18), calls=%async_computation.1 | async-start | bytes 262144 | tf_op jit(solution)/shard_map/all_to_all | solution.py:297
  45.5 10.4 %copy-start.7 = (f32[512]{0:T(512)S(1)}, f32[512]{0:T(512)}, u32[]{:S(2)}) copy-start(f32[512]{0:T(512)} %param.14) | copy-start | bytes 6148
  45.5 10.4 %copy-start = (bf16[256,512]{1,0:T(8,128)(2,1)S(1)}, bf16[256,512]{1,0:T(8,128)(2,1)}, u32[]{:S(2)}) copy-start(bf16[256,512]{1,0:T(8,128)(2,1)} %key_hbm.1) | copy-start | bytes 786436
  45.5 10.4 %copy-start.1 = (bf16[256,512]{1,0:T(8,128)(2,1)S(1)}, bf16[256,512]{1,0:T(8,128)(2,1)}, u32[]{:S(2)}) copy-start(bf16[256,512]{1,0:T(8,128)(2,1)} %value_hbm.1) | copy-start | bytes 786436
  45.6 10.4 %copy-start.9 = (s32[8]{0:T(128)S(1)}, s32[8]{0:T(128)}, u32[]{:S(2)}) copy-start(s32[8]{0:T(128)} %starts_ref.1) | copy-start | bytes 100
  45.6 10.4 %copy-start.10 = (s32[8]{0:T(128)S(1)}, s32[8]{0:T(128)}, u32[]{:S(2)}) copy-start(s32[8]{0:T(128)} %domains_ref.1) | copy-start | bytes 100
  45.6 16.3 %collective-permute-start.3 = (bf16[2,256,256]{2,1,0:T(8,128)(2,1)S(1)}, bf16[2,256,256]{2,1,0:T(8,128)(2,1)S(1)}, u32[]{:S(2)}, u32[]{:S(2)}) collective-permute-start(bf16[2,256,256]{2,1,0:T(8,128)(2,1)S(1)} %pad_maximum_fusion.refs_1_), channel_id=1, source_target_pairs={{0,3},{1,0},{2,1},{3,2},{4,7},{5,4},{6,5},{7,6},{8,11},{9,8},{10,9... | collective-permute-start | bytes 786440 | tf_op jit(solution)/shard_map/ppermute | solution.py:274
  50.4 12.6 %collective-permute-start.2 = (bf16[2,256,256]{2,1,0:T(8,128)(2,1)S(1)}, bf16[2,256,256]{2,1,0:T(8,128)(2,1)S(1)}, u32[]{:S(2)}, u32[]{:S(2)}) collective-permute-start(bf16[2,256,256]{2,1,0:T(8,128)(2,1)S(1)} %pad_maximum_fusion.refs_1_), channel_id=1, source_target_pairs={{0,2},{1,3},{2,0},{3,1},{4,6},{5,7},{6,4},{7,5},{8,10},{9,11},{10,... | collective-permute-start | bytes 786440 | tf_op jit(solution)/shard_map/ppermute | solution.py:274
  53.1 14.4 %collective-permute-start.1 = (bf16[2,256,256]{2,1,0:T(8,128)(2,1)S(1)}, bf16[2,256,256]{2,1,0:T(8,128)(2,1)S(1)}, u32[]{:S(2)}, u32[]{:S(2)}) collective-permute-start(bf16[2,256,256]{2,1,0:T(8,128)(2,1)S(1)} %pad_maximum_fusion.refs_1_), channel_id=1, source_target_pairs={{0,1},{1,2},{2,3},{3,0},{4,5},{5,6},{6,7},{7,4},{8,9},{9,10},{10,1... | collective-permute-start | bytes 786440 | tf_op jit(solution)/shard_map/ppermute | solution.py:274
  94.4 15.1 %copy-start.4 = (f32[512,16]{0,1:T(8,128)S(1)}, f32[512,16]{0,1:T(8,128)}, u32[]{:S(2)}) copy-start(f32[512,16]{0,1:T(8,128)} %param.19) | copy-start | bytes 98308
  94.4 15.1 %copy-start.5 = (f32[512,16]{0,1:T(8,128)S(1)}, f32[512,16]{0,1:T(8,128)}, u32[]{:S(2)}) copy-start(f32[512,16]{0,1:T(8,128)} %param.20) | copy-start | bytes 98308
  94.4 15.1 %copy-start.6 = (f32[512,16]{0,1:T(8,128)S(1)}, f32[512,16]{0,1:T(8,128)}, u32[]{:S(2)}) copy-start(f32[512,16]{0,1:T(8,128)} %param.21) | copy-start | bytes 98308

commit v7 on v6

--- a/solution.py
+++ b/solution.py
@@ -109,9 +109,8 @@
             rest = state - high.astype(f32)
             middle = rest.astype(bf16)
             low = (rest - middle.astype(f32)).astype(bf16)
-            summed = dot(joined, high, ((1,), (0,)))
-            summed = summed + dot(joined, middle, ((1,), (0,)))
-            summed = summed + dot(joined, low, ((1,), (0,)))
+            parts = jnp.concatenate([high, middle, low], axis=0)
+            summed = dot(jnp.concatenate([joined] * 3, axis=1), parts, ((1,), (0,)))
             total_ref[:, row * heads + head, :] = summed
     carried_ref[...] = total_ref[...].astype(bf16)
     own = lax.axis_index("chip") * 2 + lax.axis_index("core")

time: 111 us -> 111 us (level)
  no operation moved by 1% of the time
where the time goes in v7:
time: 111 us; the launch traced here: 110 us
  blocking collectives  42.7 us (38%)
  starting transfers between devices  36.5 us (33%)
  waiting for transfers between devices  21.3 us (19%)
  Pallas kernels  8.59 us (8%)
    all_to_all x1, blocking collectives, on_device(): lax.all_to_all(partial.reshape(side, side * owned, width), ('chip', 'core...  25.4 us
    all_to_all x1, starting transfers between devices, on_device(): states = lax.all_to_all(states, ('chip', 'core'), 0, 0, tiled=True)  17.5 us
    all_to_all x1, blocking collectives, on_device(): lax.all_to_all(partial.reshape(side, owned, width), ('chip', 'core'), 0,...  15.1 us
    all_to_all x1, waiting for transfers between devices, on_device(): states = lax.all_to_all(states, ('chip', 'core'), 0, 0, tiled=True)  13.9 us
    ppermute x3, starting transfers between devices, on_device(): lax.ppermute(halves, 'group', [(g, (g + k) % groups) for g in range(group...  10.3 us
    ppermute x3, waiting for transfers between devices, on_device(): lax.ppermute(halves, 'group', [(g, (g + k) % groups) for g in range(group...  7.18 us
    all_to_all x1, starting transfers between devices, on_device(): carried = lax.all_to_all(carried, ('chip', 'core'), 0, 0, tiled=True)  6.68 us
    pallas_call x1, Pallas kernels, on_device(): carried, weight_in = carry_call(domain_weights.reshape(1, -1), states)  2.29 us
  transfers between devices with their start and end apart: 6, of which 5 were waited for; matrix products, arithmetic and copies ran while one was open for 0% of the time, Pallas kernels for 4%

profile of v7, /device:TPU:8, one launch (start us, length us, event | category | flops | bytes accessed | tf_op | source)
XLA Modules:
  0.0 110.1 jit_solution(11324025960548708163)
XLA Ops:
  0.6 2.1 %state.1 = f32[128,1,640]{2,1,0:T(1,128)} custom-call(bf16[256,512]{1,0:T(8,128)(2,1)} %key_hbm.1, bf16[256,512]{1,0:T(8,128)(2,1)} %value_hbm.1, s32[1,8]{1,0:T(1,128)} %bitcast.24, s32[1,8]{1,0:T(1,128)} %bitcast.25), custom_call_target="tpu_custom_call" | custom-call | tf_op jit(solution)/shard_map/state/pallas_call | solution.py:251
  2.8 0.0 copy-start.2
  2.8 17.5 %all-to-all-start = ((f32[128,1,640]{2,1,0:T(1,128)}), f32[128,1,640]{2,1,0:T(1,128)S(1)}, u32[]{:S(2)}, u32[]{:S(2)}) async-start(f32[128,1,640]{2,1,0:T(1,128)} %state.1), calls=%async_computation | async-start | bytes 655360 | tf_op jit(solution)/shard_map/all_to_all | solution.py:268
  20.3 0.0 copy-done.2
  20.3 0.1 turn.1
  20.5 0.0 copy-start.8
  20.5 2.0 %collective-permute-start = (bf16[256,256]{1,0:T(8,128)(2,1)S(1)}, bf16[256,256]{1,0:T(8,128)(2,1)S(1)}, u32[]{:S(2)}, u32[]{:S(2)}) collective-permute-start(bf16[256,256]{1,0:T(8,128)(2,1)S(1)} %get-tuple-element.22), channel_id=1, source_target_pairs={{0,4},{4,0},{1,5},{5,1},{2,6},{6,2},{3,7},{7,3},{8,12},{12,8},{9,1... | collective-permute-start | bytes 393224 | tf_op jit(solution)/shard_map/ppermute | solution.py:269
  22.5 13.9 %all-to-all-done.states_ref = f32[128,1,640]{2,1,0:T(1,128)S(1)} async-done(((f32[128,1,640]{2,1,0:T(1,128)}), f32[128,1,640]{2,1,0:T(1,128)S(1)}, u32[]{:S(2)}, u32[]{:S(2)}) %all-to-all-start) | async-done | bytes 327712 | tf_op jit(solution)/shard_map/all_to_all | solution.py:268
  36.4 0.0 copy-done.8
  36.4 2.3 %carry.1 = (bf16[128,4,128]{2,1,0:T(4,128)(2,1)}, f32[8,128]{1,0:T(8,128)S(1)}) custom-call(s32[1,8]{1,0:T(1,128)S(1)} %bitcast.23, f32[128,1,640]{2,1,0:T(1,128)S(1)} %all-to-all-done.states_ref), custom_call_target="tpu_custom_call" | custom-call | tf_op jit(solution)/shard_map/carry/pallas_call | solution.py:295
  38.7 0.0 copy-start.3
  38.7 6.7 %all-to-all-start.1 = ((bf16[128,4,128]{2,1,0:T(4,128)(2,1)}), bf16[128,4,128]{2,1,0:T(4,128)(2,1)S(1)}, u32[]{:S(2)}, u32[]{:S(2)}) async-start(bf16[128,4,128]{2,1,0:T(4,128)(2,1)} %get-tuple-element.18), calls=%async_computation.1 | async-start | bytes 262144 | tf_op jit(solution)/shard_map/all_to_all | solution.py:296
  45.4 0.0 collective-permute-done
  45.4 0.0 copy-start.7
  45.4 0.0 copy-start
  45.4 0.0 copy-start.1
  45.5 0.0 copy-start.9
  45.5 0.0 copy-start.10
  45.5 4.8 %collective-permute-start.3 = (bf16[2,256,256]{2,1,0:T(8,128)(2,1)S(1)}, bf16[2,256,256]{2,1,0:T(8,128)(2,1)S(1)}, u32[]{:S(2)}, u32[]{:S(2)}) collective-permute-start(bf16[2,256,256]{2,1,0:T(8,128)(2,1)S(1)} %pad_maximum_fusion.refs_1_), channel_id=1, source_target_pairs={{0,3},{1,0},{2,1},{3,2},{4,7},{5,4},{6,5},{7,6},{8,11},{9,8},{10,9... | collective-permute-start | bytes 786440 | tf_op jit(solution)/shard_map/ppermute | solution.py:273
  50.3 2.7 %collective-permute-start.2 = (bf16[2,256,256]{2,1,0:T(8,128)(2,1)S(1)}, bf16[2,256,256]{2,1,0:T(8,128)(2,1)S(1)}, u32[]{:S(2)}, u32[]{:S(2)}) collective-permute-start(bf16[2,256,256]{2,1,0:T(8,128)(2,1)S(1)} %pad_maximum_fusion.refs_1_), channel_id=1, source_target_pairs={{0,2},{1,3},{2,0},{3,1},{4,6},{5,7},{6,4},{7,5},{8,10},{9,11},{10,... | collective-permute-start | bytes 786440 | tf_op jit(solution)/shard_map/ppermute | solution.py:273
  53.0 2.8 %collective-permute-start.1 = (bf16[2,256,256]{2,1,0:T(8,128)(2,1)S(1)}, bf16[2,256,256]{2,1,0:T(8,128)(2,1)S(1)}, u32[]{:S(2)}, u32[]{:S(2)}) collective-permute-start(bf16[2,256,256]{2,1,0:T(8,128)(2,1)S(1)} %pad_maximum_fusion.refs_1_), channel_id=1, source_target_pairs={{0,1},{1,2},{2,3},{3,0},{4,5},{5,6},{6,7},{7,4},{8,9},{9,10},{10,1... | collective-permute-start | bytes 786440 | tf_op jit(solution)/shard_map/ppermute | solution.py:273
  55.8 0.0 copy-done.3
  55.9 0.0 copy-done.7
  55.9 0.0 copy-done
  55.9 0.0 copy-done.1
  55.9 0.0 copy-done.9
  55.9 0.0 copy-done.10
  55.9 1.2 %inner.1 = (f32[256,512]{1,0:T(8,128)S(1)}, bf16[256,512]{1,0:T(8,128)(2,1)S(1)}, f32[8,512]{1,0:T(8,128)S(1)}) custom-call(bf16[256,512]{1,0:T(8,128)(2,1)S(1)} %copy-done.3, bf16[256,512]{1,0:T(8,128)(2,1)S(1)} %copy-done, bf16[256,512]{1,0:T(8,128)(2,1)S(1)} %copy-done.1, f32[1,512]{1,0:T(1,128)S(1)} %bitcast.22, s32[8]{0:T(128)S(1)} %copy-done.9, ...), custom_call_target="tpu_custom_call" | custom-call | tf_op jit(solution)/shard_map/inner/pallas_call | solution.py:282
  57.1 0.3 all-to-all-done.1.carried_ref
  57.4 0.6 attention.1
  58.0 2.2 %all-gather = bf16[544,512]{1,0:T(8,128)(2,1)S(1)} all-gather(bf16[272,512]{1,0:T(8,128)(2,1)S(1)} %attention.1), channel_id=2, replica_groups=mesh['chip'=64,'core'=2,'group'=4] {'core'}, dimensions={0}, use_global_device_ids=true | all-gather | bytes 835584 | tf_op jit(solution)/shard_map/all_gather | solution.py:304
  60.2 1.6 %collective-permute-done.3.refs_4_ = bf16[2,256,256]{2,1,0:T(8,128)(2,1)S(1)} collective-permute-done((bf16[2,256,256]{2,1,0:T(8,128)(2,1)S(1)}, bf16[2,256,256]{2,1,0:T(8,128)(2,1)S(1)}, u32[]{:S(2)}, u32[]{:S(2)}) %collective-permute-start.3) | collective-permute-done | bytes 262176 | tf_op jit(solution)/shard_map/ppermute | solution.py:273
  61.8 1.1 %collective-permute-done.2.refs_3_ = bf16[2,256,256]{2,1,0:T(8,128)(2,1)S(1)} collective-permute-done((bf16[2,256,256]{2,1,0:T(8,128)(2,1)S(1)}, bf16[2,256,256]{2,1,0:T(8,128)(2,1)S(1)}, u32[]{:S(2)}, u32[]{:S(2)}) %collective-permute-start.2) | collective-permute-done | bytes 262176 | tf_op jit(solution)/shard_map/ppermute | solution.py:273
  62.9 4.4 %collective-permute-done.1.refs_2_ = bf16[2,256,256]{2,1,0:T(8,128)(2,1)S(1)} collective-permute-done((bf16[2,256,256]{2,1,0:T(8,128)(2,1)S(1)}, bf16[2,256,256]{2,1,0:T(8,128)(2,1)S(1)}, u32[]{:S(2)}, u32[]{:S(2)}) %collective-permute-start.1) | collective-permute-done | bytes 262176 | tf_op jit(solution)/shard_map/ppermute | solution.py:273
  67.4 1.4 %gradient.1 = (bf16[1024,512]{1,0:T(8,128)(2,1)S(1)}, bf16[256,512]{1,0:T(8,128)(2,1)}) custom-call(bf16[2,272,512]{2,1,0:T(8,128)(2,1)S(1)} %bitcast.15, bf16[2,256,256]{2,1,0:T(8,128)(2,1)S(1)} %pad_maximum_fusion.refs_1_, bf16[2,256,256]{2,1,0:T(8,128)(2,1)S(1)} %collective-permute-done.1.refs_2_, ...), custom_call_target="tpu_custom_call" | custom-call | tf_op jit(solution)/shard_map/gradient/pallas_call | solution.py:306
  68.8 25.4 %all_to_all.20.parts_ref = bf16[8,128,512]{2,1,0:T(8,128)(2,1)S(1)} all-to-all(bf16[8,128,512]{2,1,0:T(8,128)(2,1)S(1)} %bitcast.16), channel_id=1, replica_groups={{0,8,16,24,32,40,48,56},{64,72,80,88,96,104,112,120},{128,136,144,152,1..., dimensions={0} | all-to-all | bytes 2097152 | tf_op jit(solution)/shard_map/all_to_all | solution.py:319
  94.2 0.1 sum.1
  94.3 0.0 copy-start.4
  94.3 0.0 copy-start.5
  94.4 0.0 copy-start.6
  94.4 15.1 %all_to_all.21.parts_ref = bf16[8,16,512]{2,1,0:T(8,128)(2,1)S(1)} all-to-all(bf16[8,16,512]{2,1,0:T(8,128)(2,1)S(1)} %bitcast.17), channel_id=1, replica_groups={{0,64,128,192,256,320,384,448},{8,72,136,200,264,328,392,456},{16,80,14..., dimensions={0} | all-to-all | bytes 262144 | tf_op jit(solution)/shard_map/all_to_all | solution.py:328
  109.4 0.0 copy-done.4
  109.5 0.0 copy-done.5
  109.5 0.0 copy-done.6
  109.5 0.7 update.1
  (1 shorter events, 0.0 us)
Async XLA Ops:
  2.8 17.5 %copy-start.2 = (bf16[256,512]{1,0:T(8,128)(2,1)S(1)}, bf16[256,512]{1,0:T(8,128)(2,1)}, u32[]{:S(2)}) copy-start(bf16[256,512]{1,0:T(8,128)(2,1)} %refs_0_.1) | copy-start | bytes 786436
  2.8 33.6 %all-to-all-start = ((f32[128,1,640]{2,1,0:T(1,128)}), f32[128,1,640]{2,1,0:T(1,128)S(1)}, u32[]{:S(2)}, u32[]{:S(2)}) async-start(f32[128,1,640]{2,1,0:T(1,128)} %state.1), calls=%async_computation | async-start | bytes 655360 | tf_op jit(solution)/shard_map/all_to_all | solution.py:268
  20.5 16.0 %copy-start.8 = (s32[8]{0:T(128)S(1)}, s32[8]{0:T(128)}, u32[]{:S(2)}) copy-start(s32[8]{0:T(128)} %weights_ref.1) | copy-start | bytes 100
  20.5 24.9 %collective-permute-start = (bf16[256,256]{1,0:T(8,128)(2,1)S(1)}, bf16[256,256]{1,0:T(8,128)(2,1)S(1)}, u32[]{:S(2)}, u32[]{:S(2)}) collective-permute-start(bf16[256,256]{1,0:T(8,128)(2,1)S(1)} %get-tuple-element.22), channel_id=1, source_target_pairs={{0,4},{4,0},{1,5},{5,1},{2,6},{6,2},{3,7},{7,3},{8,12},{12,8},{9,1... | collective-permute-start | bytes 393224 | tf_op jit(solution)/shard_map/ppermute | solution.py:269
  38.7 17.1 %copy-start.3 = (bf16[256,512]{1,0:T(8,128)(2,1)S(1)}, bf16[256,512]{1,0:T(8,128)(2,1)}, u32[]{:S(2)}) copy-start(bf16[256,512]{1,0:T(8,128)(2,1)} %query_ref.1) | copy-start | bytes 786436
  38.7 18.7 %all-to-all-start.1 = ((bf16[128,4,128]{2,1,0:T(4,128)(2,1)}), bf16[128,4,128]{2,1,0:T(4,128)(2,1)S(1)}, u32[]{:S(2)}, u32[]{:S(2)}) async-start(bf16[128,4,128]{2,1,0:T(4,128)(2,1)} %get-tuple-element.18), calls=%async_computation.1 | async-start | bytes 262144 | tf_op jit(solution)/shard_map/all_to_all | solution.py:296
  45.4 10.4 %copy-start.7 = (f32[512]{0:T(512)S(1)}, f32[512]{0:T(512)}, u32[]{:S(2)}) copy-start(f32[512]{0:T(512)} %param.14) | copy-start | bytes 6148
  45.4 10.4 %copy-start = (bf16[256,512]{1,0:T(8,128)(2,1)S(1)}, bf16[256,512]{1,0:T(8,128)(2,1)}, u32[]{:S(2)}) copy-start(bf16[256,512]{1,0:T(8,128)(2,1)} %key_hbm.1) | copy-start | bytes 786436
  45.4 10.4 %copy-start.1 = (bf16[256,512]{1,0:T(8,128)(2,1)S(1)}, bf16[256,512]{1,0:T(8,128)(2,1)}, u32[]{:S(2)}) copy-start(bf16[256,512]{1,0:T(8,128)(2,1)} %value_hbm.1) | copy-start | bytes 786436
  45.5 10.4 %copy-start.9 = (s32[8]{0:T(128)S(1)}, s32[8]{0:T(128)}, u32[]{:S(2)}) copy-start(s32[8]{0:T(128)} %starts_ref.1) | copy-start | bytes 100
  45.5 10.4 %copy-start.10 = (s32[8]{0:T(128)S(1)}, s32[8]{0:T(128)}, u32[]{:S(2)}) copy-start(s32[8]{0:T(128)} %domains_ref.1) | copy-start | bytes 100
  45.5 16.3 %collective-permute-start.3 = (bf16[2,256,256]{2,1,0:T(8,128)(2,1)S(1)}, bf16[2,256,256]{2,1,0:T(8,128)(2,1)S(1)}, u32[]{:S(2)}, u32[]{:S(2)}) collective-permute-start(bf16[2,256,256]{2,1,0:T(8,128)(2,1)S(1)} %pad_maximum_fusion.refs_1_), channel_id=1, source_target_pairs={{0,3},{1,0},{2,1},{3,2},{4,7},{5,4},{6,5},{7,6},{8,11},{9,8},{10,9... | collective-permute-start | bytes 786440 | tf_op jit(solution)/shard_map/ppermute | solution.py:273
  50.3 12.6 %collective-permute-start.2 = (bf16[2,256,256]{2,1,0:T(8,128)(2,1)S(1)}, bf16[2,256,256]{2,1,0:T(8,128)(2,1)S(1)}, u32[]{:S(2)}, u32[]{:S(2)}) collective-permute-start(bf16[2,256,256]{2,1,0:T(8,128)(2,1)S(1)} %pad_maximum_fusion.refs_1_), channel_id=1, source_target_pairs={{0,2},{1,3},{2,0},{3,1},{4,6},{5,7},{6,4},{7,5},{8,10},{9,11},{10,... | collective-permute-start | bytes 786440 | tf_op jit(solution)/shard_map/ppermute | solution.py:273
  53.0 14.4 %collective-permute-start.1 = (bf16[2,256,256]{2,1,0:T(8,128)(2,1)S(1)}, bf16[2,256,256]{2,1,0:T(8,128)(2,1)S(1)}, u32[]{:S(2)}, u32[]{:S(2)}) collective-permute-start(bf16[2,256,256]{2,1,0:T(8,128)(2,1)S(1)} %pad_maximum_fusion.refs_1_), channel_id=1, source_target_pairs={{0,1},{1,2},{2,3},{3,0},{4,5},{5,6},{6,7},{7,4},{8,9},{9,10},{10,1... | collective-permute-start | bytes 786440 | tf_op jit(solution)/shard_map/ppermute | solution.py:273
  94.3 15.1 %copy-start.4 = (f32[512,16]{0,1:T(8,128)S(1)}, f32[512,16]{0,1:T(8,128)}, u32[]{:S(2)}) copy-start(f32[512,16]{0,1:T(8,128)} %param.19) | copy-start | bytes 98308
  94.3 15.1 %copy-start.5 = (f32[512,16]{0,1:T(8,128)S(1)}, f32[512,16]{0,1:T(8,128)}, u32[]{:S(2)}) copy-start(f32[512,16]{0,1:T(8,128)} %param.20) | copy-start | bytes 98308
  94.4 15.1 %copy-start.6 = (f32[512,16]{0,1:T(8,128)S(1)}, f32[512,16]{0,1:T(8,128)}, u32[]{:S(2)}) copy-start(f32[512,16]{0,1:T(8,128)} %param.21) | copy-start | bytes 98308
